TPU v7x, 32 devices: a whole 2x2x4 slice. The times are simulated.
32 devices in a mesh: batch: 8 (over z, y), head: 4 (over x, core).
Axes of the slice: x: 2, y: 2, z: 4, core: 2. Of those that a mesh axis runs over, the one named last changes fastest.
Arguments:
- inputs: bfloat16 [8192, 768], P(('batch', 'head')), may hold values from -6 to 6
- bucket: int32 [16], P('batch'), may hold values from 0 to 1, as said below
- lengths: int32 [16, 4], P('batch'), may hold values from 0 to 512, as said below
- qkv_weight: bfloat16 [768, 2304], P(None, ('batch', 'head')), may hold values from -0.21875 to 0.21875
- query_bias: bfloat16 [768], P(('batch', 'head')), may hold values from -3 to 3
- value_bias: bfloat16 [768], P(('batch', 'head')), may hold values from -3 to 3
- proj_weight: bfloat16 [768, 768], P(None, ('batch', 'head')), may hold values from -1.75 to 1.75
- proj_bias: bfloat16 [768], P(('batch', 'head')), may hold values from -3 to 3
- first_gain: bfloat16 [768], P(('batch', 'head')), may hold values from 0.099609375 to 1.8984375
- first_shift: bfloat16 [768], P(('batch', 'head')), may hold values from -2 to 2
- up_weight: bfloat16 [768, 3072], P(None, ('batch', 'head')), may hold values from -0.21875 to 0.21875
- up_bias: bfloat16 [3072], P(('batch', 'head')), may hold values from -3 to 3
- down_weight: bfloat16 [3072, 768], P(('batch', 'head')), may hold values from -0.109375 to 0.109375
- down_bias: bfloat16 [768], P(('batch', 'head')), may hold values from -3 to 3
- second_gain: bfloat16 [768], P(('batch', 'head')), may hold values from 0.099609375 to 1.8984375
- second_shift: bfloat16 [768], P(('batch', 'head')), may hold values from -2 to 2
- cotangent: bfloat16 [8192, 768], P(('batch', 'head')), may hold values from -6 to 6
Outputs:
- layer_out: bfloat16 [8192, 768], P(('batch', 'head'))
- inputs_grad: bfloat16 [8192, 768], P(('batch', 'head'))
- qkv_grad: float32 [768, 2304], P('batch', 'head')
- qbias_grad: float32 [768], P(('batch', 'head'))
- vbias_grad: float32 [768], P(('batch', 'head'))
- proj_grad: float32 [768, 768], P('head', 'batch')
- pbias_grad: float32 [768], P(('batch', 'head'))
- fgain_grad: float32 [768], P(('batch', 'head'))
- fshift_grad: float32 [768], P(('batch', 'head'))
- up_grad: float32 [768, 3072], P(None, ('batch', 'head'))
- ubias_grad: float32 [3072], P(('batch', 'head'))
- down_grad: float32 [3072, 768], P(('batch', 'head'))
- dbias_grad: float32 [768], P(('batch', 'head'))
- sgain_grad: float32 [768], P(('batch', 'head'))
- sshift_grad: float32 [768], P(('batch', 'head'))
Inputs may be any that keep to these rules, and one draw needn't show every extreme that they name: `bucket`: 1 marks a block holding one sequence of up to 512 tokens, 0 a block holding 4 sequences, one in each aligned block of 128 rows. For a block marked 1, entry 0 is its sequence's length, over 128, and the other entries are 0; for a block marked 0, entry u is the length of the sequence starting at row u * 128, 1 to 128; lengths 512 and 128 occur.
All inputs are finite; a program needn't handle non-finite values.
Results may differ from a plain program's by a relative error of at most 0.017.
Values may be sent and summed in bfloat16 or wider, within the bound.
No kernel may reach another device: no remote copies, remote signals or barrier semaphores. Data moves between devices by JAX's collectives and lax.ppermute only.
A program may use at most 128 MiB of HBM per device.

v0:
```python
import jax
import jax.numpy as jnp
from jax import lax
from jax.sharding import PartitionSpec as P

D = 768
HEADS = 12
HEAD_DIM = 64
FF = 3072
BIG = 512
SMALL = 128
UNITS = 4


NORM_EPS = 1e-12


def layer_norm(values, gain, shift):
    center = values - jnp.mean(values, -1, keepdims=True)
    spread = jnp.mean(center * center, -1, keepdims=True)
    return center * lax.rsqrt(spread + NORM_EPS) * gain + shift


def gelu_exact(values):
    return jax.nn.gelu(values, approximate=False)


def block_masks(bucket, lengths):
    units = jnp.arange(UNITS, dtype=jnp.int32)
    long_live = jnp.clip(lengths[:, :1] - SMALL * units[None, :], 0, SMALL)
    unit_live = jnp.where(bucket[:, None] == 1, long_live, lengths)
    places = jnp.arange(BIG, dtype=jnp.int32)
    unit_of = places // SMALL
    inner = places - unit_of * SMALL
    live_rows = inner[None, :] < jnp.repeat(unit_live, SMALL, axis=1)
    segments = jnp.where(bucket[:, None] == 1, 0, unit_of[None, :])
    return (live_rows, segments)


def masked_scores(query, keys, live_row, segment):
    allowed = (segment[:, None] == segment[None, :]) & live_row[None, :]
    scores = jnp.einsum(
        "qhd,khd->hqk", query, keys, preferred_element_type=jnp.float32
    ) * HEAD_DIM ** (-0.5)
    return jnp.where(allowed[None], scores, -1e30)


def attend_forward(packed):
    query, keys, values, live_row, segment = packed
    scores = masked_scores(query, keys, live_row, segment)
    highest = jnp.max(scores, -1, keepdims=True)
    exp_vals = jnp.exp(scores - highest)
    totals = jnp.sum(exp_vals, -1, keepdims=True)
    probs = exp_vals / totals
    context = jnp.einsum(
        "hqk,khd->qhd", probs.astype(jnp.bfloat16), values, preferred_element_type=jnp.float32
    )
    return (context.astype(jnp.bfloat16), highest + jnp.log(totals))


def attend_backward(packed):
    query, keys, values, live_row, segment, ctx_cot, log_total = packed
    scores = masked_scores(query, keys, live_row, segment)
    probs = jnp.exp(scores - log_total)
    probs_low = probs.astype(jnp.bfloat16)
    value_cot = jnp.einsum("hqk,qhd->khd", probs_low, ctx_cot, preferred_element_type=jnp.float32)
    prob_cot = jnp.einsum("qhd,khd->hqk", ctx_cot, values, preferred_element_type=jnp.float32)
    score_cot = (probs * (prob_cot - jnp.sum(probs * prob_cot, -1, keepdims=True))).astype(
        jnp.bfloat16
    )
    query_cot = jnp.einsum(
        "hqk,khd->qhd", score_cot, keys, preferred_element_type=jnp.float32
    ) * HEAD_DIM ** (-0.5)
    keys_cot = jnp.einsum(
        "hqk,qhd->khd", score_cot, query, preferred_element_type=jnp.float32
    ) * HEAD_DIM ** (-0.5)
    return jnp.stack([query_cot, keys_cot, value_cot], axis=2).astype(jnp.bfloat16)


def local(
    inputs,
    bucket,
    lengths,
    qkv_weight,
    query_bias,
    value_bias,
    proj_weight,
    proj_bias,
    first_gain,
    first_shift,
    up_weight,
    up_bias,
    down_weight,
    down_bias,
    second_gain,
    second_shift,
    cotangent,
):
    head_count = lax.axis_size("head")
    batch_count = lax.axis_size("batch")
    head_place = lax.axis_index("head")
    row_count = inputs.shape[0]
    group_rows = row_count * head_count
    block_count = group_rows // BIG
    local_heads = HEADS // head_count
    local_width = local_heads * HEAD_DIM
    unit_width = FF // (batch_count * head_count)
    local_units = batch_count * unit_width
    (
        qkv_full,
        qbias_full,
        vbias_full,
        proj_full,
        pbias_full,
        fgain_full,
        fshift_full,
        up_full,
        ubias_full,
        down_full,
        dbias_full,
        sgain_full,
        sshift_full,
    ) = (
        lax.all_gather(qkv_weight, ("batch", "head"), axis=1, tiled=True),
        lax.all_gather(query_bias, ("batch", "head"), axis=0, tiled=True),
        lax.all_gather(value_bias, ("batch", "head"), axis=0, tiled=True),
        lax.all_gather(proj_weight, ("batch", "head"), axis=1, tiled=True),
        lax.all_gather(proj_bias, ("batch", "head"), axis=0, tiled=True),
        lax.all_gather(first_gain, ("batch", "head"), axis=0, tiled=True),
        lax.all_gather(first_shift, ("batch", "head"), axis=0, tiled=True),
        lax.all_gather(up_weight, ("batch", "head"), axis=1, tiled=True),
        lax.all_gather(up_bias, ("batch", "head"), axis=0, tiled=True),
        lax.all_gather(down_weight, ("batch", "head"), axis=0, tiled=True),
        lax.all_gather(down_bias, ("batch", "head"), axis=0, tiled=True),
        lax.all_gather(second_gain, ("batch", "head"), axis=0, tiled=True),
        lax.all_gather(second_shift, ("batch", "head"), axis=0, tiled=True),
    )
    fgain = fgain_full.astype(jnp.float32)
    fshift = fshift_full.astype(jnp.float32)
    sgain = sgain_full.astype(jnp.float32)
    sshift = sshift_full.astype(jnp.float32)
    live_rows, segments = block_masks(bucket, lengths)
    own_live = lax.dynamic_slice_in_dim(live_rows.reshape(-1), head_place * row_count, row_count)
    group_in = lax.all_gather(inputs, "head", axis=0, tiled=True)
    qkv_own = lax.dynamic_slice_in_dim(qkv_full, head_place * 3 * local_width, 3 * local_width, 1)
    qbias_own = lax.dynamic_slice_in_dim(qbias_full, head_place * local_width, local_width, 0)
    vbias_own = lax.dynamic_slice_in_dim(vbias_full, head_place * local_width, local_width, 0)
    projected = jnp.dot(group_in, qkv_own, preferred_element_type=jnp.float32).reshape(
        group_rows, local_heads, 3, HEAD_DIM
    )
    zero_bias = jnp.zeros((local_heads, HEAD_DIM), jnp.float32)
    bias_own = jnp.stack(
        [
            qbias_own.astype(jnp.float32).reshape(local_heads, HEAD_DIM),
            zero_bias,
            vbias_own.astype(jnp.float32).reshape(local_heads, HEAD_DIM),
        ],
        axis=1,
    )
    by_heads = (
        (projected + bias_own)
        .astype(jnp.bfloat16)
        .reshape(block_count, BIG, local_heads, 3, HEAD_DIM)
    )
    query_all = by_heads[:, :, :, 0]
    keys_all = by_heads[:, :, :, 1]
    values_all = by_heads[:, :, :, 2]
    context, log_total = lax.map(
        attend_forward, (query_all, keys_all, values_all, live_rows, segments)
    )
    context_heads = context.reshape(group_rows, local_width)
    context_tok = lax.all_to_all(context_heads, "head", split_axis=0, concat_axis=1, tiled=True)
    attn = jnp.dot(context_tok, proj_full, preferred_element_type=jnp.float32) + pbias_full.astype(
        jnp.float32
    )
    first, first_pull = jax.vjp(layer_norm, inputs.astype(jnp.float32) + attn, fgain, fshift)
    first_low = first.astype(jnp.bfloat16)
    up_val = jnp.dot(first_low, up_full, preferred_element_type=jnp.float32) + ubias_full.astype(
        jnp.float32
    )
    hidden_low = gelu_exact(up_val).astype(jnp.bfloat16)
    down = jnp.dot(hidden_low, down_full, preferred_element_type=jnp.float32) + dbias_full.astype(
        jnp.float32
    )
    result, second_pull = jax.vjp(layer_norm, first + down, sgain, sshift)
    layer_out = result.astype(jnp.bfloat16)
    qkv_back, proj_back, up_back, down_back = (
        lax.all_gather(qkv_weight, ("batch", "head"), axis=1, tiled=True),
        lax.all_gather(proj_weight, ("batch", "head"), axis=1, tiled=True),
        lax.all_gather(up_weight, ("batch", "head"), axis=1, tiled=True),
        lax.all_gather(down_weight, ("batch", "head"), axis=0, tiled=True),
    )
    out_cot = cotangent.astype(jnp.float32) * own_live[:, None].astype(jnp.float32)
    sum_two_cot, sgain_grad, sshift_grad = second_pull(out_cot)
    down_cot = sum_two_cot.astype(jnp.bfloat16)
    dbias_grad = jnp.sum(down_cot, 0, dtype=jnp.float32)
    first_group, down_group = (
        lax.all_gather(first_low, "head", axis=0, tiled=True),
        lax.all_gather(down_cot, "head", axis=0, tiled=True),
    )
    up_sel = lax.dynamic_slice_in_dim(
        up_back.reshape(D, batch_count, head_count, unit_width), head_place, 1, 2
    ).reshape(D, local_units)
    ubias_sel = lax.dynamic_slice_in_dim(
        ubias_full.reshape(batch_count, head_count, unit_width), head_place, 1, 1
    ).reshape(local_units)
    down_sel = lax.dynamic_slice_in_dim(
        down_back.reshape(batch_count, head_count, unit_width, D), head_place, 1, 1
    ).reshape(local_units, D)
    up_cols = jnp.dot(first_group, up_sel, preferred_element_type=jnp.float32) + ubias_sel.astype(
        jnp.float32
    )
    hidden_cols, gelu_pull = jax.vjp(gelu_exact, up_cols)
    hidden_cols_low = hidden_cols.astype(jnp.bfloat16)
    hidden_cot = jnp.einsum("rd,fd->rf", down_group, down_sel, preferred_element_type=jnp.float32)
    up_cot = gelu_pull(hidden_cot)[0].astype(jnp.bfloat16)
    down_grad = jnp.einsum(
        "rf,rd->fd", hidden_cols_low, down_group, preferred_element_type=jnp.float32
    )
    up_grad = jnp.einsum("rd,rf->df", first_group, up_cot, preferred_element_type=jnp.float32)
    ubias_grad = jnp.sum(up_cot, 0, dtype=jnp.float32)
    ffn_cot = lax.psum_scatter(
        jnp.einsum("rf,df->rd", up_cot, up_sel, preferred_element_type=jnp.float32).astype(
            jnp.bfloat16
        ),
        "head",
        scatter_dimension=0,
        tiled=True,
    ).astype(jnp.float32)
    first_cot = sum_two_cot + ffn_cot
    sum_one_cot, fgain_grad, fshift_grad = first_pull(first_cot)
    attn_cot = sum_one_cot.astype(jnp.bfloat16)
    pbias_grad = jnp.sum(attn_cot, 0, dtype=jnp.float32)
    attn_group = lax.all_gather(attn_cot, "head", axis=0, tiled=True)
    proj_own = lax.dynamic_slice_in_dim(proj_back, head_place * local_width, local_width, 0)
    proj_grad = jnp.einsum(
        "rc,rd->cd", context_heads, attn_group, preferred_element_type=jnp.float32
    )
    context_cot = jnp.einsum(
        "rd,cd->rc", attn_group, proj_own, preferred_element_type=jnp.float32
    ).astype(jnp.bfloat16)
    cot_blocks = context_cot.reshape(block_count, BIG, local_heads, HEAD_DIM)
    qkv_cot = lax.map(
        attend_backward,
        (query_all, keys_all, values_all, live_rows, segments, cot_blocks, log_total),
    )
    qkv_heads = qkv_cot.reshape(group_rows, 3 * local_width)
    qkv_grad = jnp.einsum("rd,rc->dc", group_in, qkv_heads, preferred_element_type=jnp.float32)
    back_tok = lax.all_to_all(
        qkv_heads.reshape(group_rows, 1, 3 * local_width),
        "head",
        split_axis=0,
        concat_axis=1,
        tiled=True,
    )
    back_tok = back_tok.reshape(row_count, 3 * D)
    back_split = back_tok.reshape(row_count, HEADS, 3, HEAD_DIM)
    qbias_grad = jnp.sum(back_split[:, :, 0, :], 0, dtype=jnp.float32).reshape(D)
    vbias_grad = jnp.sum(back_split[:, :, 2, :], 0, dtype=jnp.float32).reshape(D)
    inputs_grad = (
        sum_one_cot
        + jnp.einsum("rc,dc->rd", back_tok, qkv_back, preferred_element_type=jnp.float32)
    ).astype(jnp.bfloat16)
    big_sums = (
        lax.psum_scatter(qkv_grad, "batch", scatter_dimension=0, tiled=True),
        lax.psum_scatter(proj_grad, "batch", scatter_dimension=1, tiled=True),
        lax.psum_scatter(up_grad, "batch", scatter_dimension=1, tiled=True),
        lax.psum_scatter(ubias_grad, "batch", scatter_dimension=0, tiled=True),
        lax.psum_scatter(down_grad, "batch", scatter_dimension=0, tiled=True),
    )
    small_sums = (
        lax.psum_scatter(qbias_grad, ("batch", "head"), scatter_dimension=0, tiled=True),
        lax.psum_scatter(vbias_grad, ("batch", "head"), scatter_dimension=0, tiled=True),
        lax.psum_scatter(pbias_grad, ("batch", "head"), scatter_dimension=0, tiled=True),
        lax.psum_scatter(fgain_grad, ("batch", "head"), scatter_dimension=0, tiled=True),
        lax.psum_scatter(fshift_grad, ("batch", "head"), scatter_dimension=0, tiled=True),
        lax.psum_scatter(dbias_grad, ("batch", "head"), scatter_dimension=0, tiled=True),
        lax.psum_scatter(sgain_grad, ("batch", "head"), scatter_dimension=0, tiled=True),
        lax.psum_scatter(sshift_grad, ("batch", "head"), scatter_dimension=0, tiled=True),
    )
    return (
        layer_out,
        inputs_grad,
        big_sums[0],
        small_sums[0],
        small_sums[1],
        big_sums[1],
        small_sums[2],
        small_sums[3],
        small_sums[4],
        big_sums[2],
        big_sums[3],
        big_sums[4],
        small_sums[5],
        small_sums[6],
        small_sums[7],
    )


def solution(mesh):
    in_specs = (
        P(("batch", "head"), None),
        P("batch"),
        P("batch", None),
        P(None, ("batch", "head")),
        P(("batch", "head")),
        P(("batch", "head")),
        P(None, ("batch", "head")),
        P(("batch", "head")),
        P(("batch", "head")),
        P(("batch", "head")),
        P(None, ("batch", "head")),
        P(("batch", "head")),
        P(("batch", "head"), None),
        P(("batch", "head")),
        P(("batch", "head")),
        P(("batch", "head")),
        P(("batch", "head"), None),
    )
    out_specs = (
        P(("batch", "head"), None),
        P(("batch", "head"), None),
        P("batch", "head"),
        P(("batch", "head")),
        P(("batch", "head")),
        P("head", "batch"),
        P(("batch", "head")),
        P(("batch", "head")),
        P(("batch", "head")),
        P(None, ("batch", "head")),
        P(("batch", "head")),
        P(("batch", "head"), None),
        P(("batch", "head")),
        P(("batch", "head")),
        P(("batch", "head")),
    )
    return jax.shard_map(local, mesh=mesh, in_specs=in_specs, out_specs=out_specs, check_vma=False)
```

profile of v0, /device:TPU:0, one launch (start us, length us, event | category | flops | bytes accessed | tf_op | source)
XLA Modules:
  0.0 681.3 jit_solution(14542512077119066717)
XLA Ops:
  18.2 42.7 %all-reduce.19 = (bf16[3072]{0:T(1024)(128)(2,1)S(1)}, bf16[768]{0:T(1024)(128)(2,1)S(1)}, bf16[768]{0:T(1024)(128)(2,1)S(1)}, bf16[768]{0:T(1024)(128)(2,1)S(1)...) all-reduce(bf16[3072]{0:T(1024)(128)(2,1)S(1)} %dynamic-update-slic, ...), channel_id=1, replica_groups=mesh['batch'=8,'head'=4] {'batch','head'}, use_global_device_ids=true, to_apply=%add.5 | all-reduce | flops 9216 | bytes 36864
  65.5 30.3 %all-gather.9.cloned.1.call-done = bf16[768,2304]{0,1:T(8,128)(2,1)} async-done(((bf16[768,72]{0,1:T(8,128)(2,1)}), bf16[768,2304]{0,1:T(8,128)(2,1)}) %all-gather.9.cloned.1.call-update) | async-done | bytes 3538960 | tf_op jit(solution)/shard_map/all_gather | solution.py:124
  95.8 4.2 convolution_bitcast_fusion
  100.0 3.3 reshape.355
  103.9 5.8 while.22
  105.7 1.1 fusion.176
  111.1 3.5 all-to-all-start
  115.9 35.6 %all-gather.13.cloned.1.call-done = bf16[768,768]{0,1:T(8,128)(2,1)} async-done(((bf16[768,24]{0,1:T(8,128)(2,1)}), bf16[768,768]{0,1:T(8,128)(2,1)}) %all-gather.13.cloned.1.call-update) | async-done | bytes 1179664 | tf_op jit(solution)/shard_map/all_gather | solution.py:127
  151.6 1.9 fusion.128
  155.0 62.0 %all-gather.15.cloned.1.call-done = bf16[768,3072]{0,1:T(8,128)(2,1)} async-done(((bf16[768,96]{0,1:T(8,128)(2,1)}), bf16[768,3072]{0,1:T(8,128)(2,1)}) %all-gather.15.cloned.1.call-update) | async-done | bytes 4718608 | tf_op jit(solution)/shard_map/all_gather | solution.py:131
  216.9 65.2 %all-gather.17.cloned.1.call-done = bf16[3072,768]{1,0:T(8,128)(2,1)} async-done(((bf16[96,768]{1,0:T(8,128)(2,1)}), bf16[3072,768]{1,0:T(8,128)(2,1)}) %all-gather.17.cloned.1.call-update) | async-done | bytes 4718608 | tf_op jit(solution)/shard_map/all_gather | solution.py:133
  282.1 12.8 %fusion.129 = (f32[256]{0:T(256)S(1)}, f32[256,768]{1,0:T(8,128)S(1)}) fusion(f32[768]{0:T(1024)} %convert_element_type.128, bf16[3072,768]{1,0:T(8,128)(2,1)} %all-gather.17.cloned.1.call-done, f32[3072]{0:T(1024)} %convert_element_type.126, bf16[768,3072]{0,1:T(8,128)(2,1)} %all-gather.15.cloned.1.call-done, f32[256,768]{1,0:T(8,128)S(1)} %get-tuple-element.259, ...), kind=kOutput, calls=%fused_computation.213 | convolution fusion | flops 2470182656 | bytes 11034624 | tf_op jit(solution)/shard_map/dot_general | solution.py:182
  296.2 2.2 fusion.127
  298.3 1.5 convert_reduce_fusion.1
  301.0 2.4 constant_dynamic-slice_fusion.3
  303.4 2.4 constant_dynamic-slice_fusion.2
  305.7 4.8 fusion.132
  310.6 13.3 %all-gather.21.cloned.1.call-done = bf16[1024,768]{1,0:T(8,128)(2,1)} async-done(((bf16[256,768]{1,0:T(8,128)(2,1)}), bf16[1024,768]{1,0:T(8,128)(2,1)}) %all-gather.21.cloned.1.call-update) | async-done | bytes 1572880 | tf_op jit(solution)/shard_map/all_gather | solution.py:199
  323.8 12.2 %convert_reduce_fusion = (f32[768]{0:T(1024)}, bf16[1024,768]{1,0:T(8,128)(2,1)S(1)}, f32[1024,768]{1,0:T(8,128)}) fusion(f32[1024,768]{1,0:T(8,128)} %fusion.132, f32[768]{0:T(1024)S(1)} %reshape.371, bf16[1024,768]{1,0:T(8,128)(2,1)} %all-gather.21.cloned.1.call-done, bf16[768,768]{1,0:T(8,128)(2,1)} %bitcast.185), kind=kOutput, calls=%fused_computation.70 | convolution fusion | flops 1266941184 | bytes 10622976 | tf_op jit(solution)/shard_map/rd,fd->rf/dot_general | solution.py:215
  336.0 1.2 copy-done.33
  337.2 2.5 convolution_convert_fusion
  339.8 28.3 %reduce-scatter.10.cloned.1.call-done = bf16[256,768]{1,0:T(8,128)(2,1)} async-done(((bf16[1024,768]{1,0:T(8,128)(2,1)}), bf16[256,768]{1,0:T(8,128)(2,1)}) %reduce-scatter.10.cloned.1.call-update) | async-done | bytes 393232 | tf_op jit(solution)/shard_map/reduce_scatter | solution.py:222
  368.1 2.0 multiply_reduce_fusion.2
  370.2 1.4 fusion.126
  373.6 19.7 %all-gather.23.cloned.1.call-done = bf16[1024,768]{1,0:T(8,128)(2,1)} async-done(((bf16[256,768]{1,0:T(8,128)(2,1)}), bf16[1024,768]{1,0:T(8,128)(2,1)}) %all-gather.23.cloned.1.call-update) | async-done | bytes 1572880 | tf_op jit(solution)/shard_map/all_gather | solution.py:234
  393.3 3.0 convolution_bitcast_fusion.2
  396.4 5.7 fusion.66
  402.2 4.9 fusion.133
  407.5 1.9 convolution_convert_fusion.1
  409.7 11.4 %while.23 = (s32[]{:T(128)}, bf16[2,512,3,3,64]{1,4,2,3,0:T(8,128)(2,1)}, bf16[2,512,3,64]{1,3,2,0:T(8,128)(2,1)S(1)}, s32[2,512]{1,0:T(2,128)S(1)}, pred[2,512]...) while((s32[]{:T(128)}, ...), condition=%wide.region_15.16_spmd, body=%wide.region_13.15_spmd.sunk | while | flops 513178112 | bytes 36742840 | solution.py:243
  410.6 1.2 multiply_reduce_fusion.8
  416.3 1.2 multiply_reduce_fusion.8
  421.1 2.6 copy.61
  424.0 1.1 convolution_bitcast_fusion.1
  425.1 1.8 copy.74
  428.3 1.6 reduce.12
  430.6 2.6 reshape.407
  433.2 4.3 all-to-all-start.1
  438.7 21.4 %all-reduce.14 = f32[768]{0:T(1024)S(1)} all-reduce(f32[768]{0:T(1024)S(1)} %copy-done.28), channel_id=11, replica_groups=mesh['batch'=8,'head'=4] {'batch'}, use_global_device_ids=true, to_apply=%region_30.31.clone | all-reduce | flops 768 | bytes 6144
  460.7 3.5 reshape.408
  464.2 1.3 copy.78
  465.5 2.7 copy.73
  469.0 38.1 %all-reduce.18 = (f32[768]{0:T(1024)S(1)}, f32[768]{0:T(1024)S(1)}, f32[768]{0:T(1024)S(1)}, f32[768]{0:T(1024)S(1)}, f32[768]{0:T(1024)S(1)}, /*index=5*/f32[768]{0:T(1024)S(1)}, f32[768]{0:T(1024)S(1)}, f32[768]{0:T(1024)S(1)}) all-reduce(f32[768]{0:T(1024)S(1)} %reshape.366, ...), channel_id=4, replica_groups=mesh['batch'=8,'head'=4] {'batch','head'}, use_global_device_ids=true, to_apply=%region_18.19.clone | all-reduce | flops 6144 | bytes 49152
  511.8 3.9 fusion.78
  515.7 1.6 copy.77
  517.3 14.6 %reduce-scatter.14.cloned.1.call-done = f32[96,768]{1,0:T(8,128)} async-done(((f32[768,768]{1,0:T(8,128)}), f32[96,768]{1,0:T(8,128)}) %reduce-scatter.14.cloned.1.call-update) | async-done | bytes 294928 | tf_op jit(solution)/shard_map/reduce_scatter | solution.py:269
  532.0 72.4 %reduce-scatter.12.cloned.1.call-done = f32[768,96]{0,1:T(8,128)} async-done(((f32[768,768]{0,1:T(8,128)}), f32[768,96]{0,1:T(8,128)}) %reduce-scatter.12.cloned.1.call-update) | async-done | bytes 294928 | tf_op jit(solution)/shard_map/reduce_scatter | solution.py:267
  604.4 70.0 %reduce-scatter.16.cloned.1.call-done = f32[96,576]{1,0:T(8,128)} async-done(((f32[768,576]{1,0:T(8,128)}), f32[96,576]{1,0:T(8,128)}) %reduce-scatter.16.cloned.1.call-update) | async-done | bytes 221200
  (224 shorter events, 47.8 us)
Async XLA Ops:
  7.2 58.3 %all-gather.11.cloned.1.call-start = ((), (), s32[]{:S(2)}) async-start(), calls=%async_computation.8 | async-start | bytes 1966080 | tf_op jit(solution)/shard_map/all_gather | solution.py:144
  7.9 87.9 %all-gather.9.cloned.1.call-start = ((), (), s32[]{:S(2)}) async-start(), calls=%async_computation.7 | async-start | bytes 3649536 | tf_op jit(solution)/shard_map/all_gather | solution.py:124
  8.7 142.9 %all-gather.13.cloned.1.call-start = ((), (), s32[]{:S(2)}) async-start(), calls=%async_computation.9 | async-start | bytes 1216512 | tf_op jit(solution)/shard_map/all_gather | solution.py:127
  9.4 207.5 %all-gather.15.cloned.1.call-start = ((), (), s32[]{:S(2)}) async-start(), calls=%async_computation.10 | async-start | bytes 4866048 | tf_op jit(solution)/shard_map/all_gather | solution.py:131
  10.0 272.1 %all-gather.17.cloned.1.call-start = ((), (), s32[]{:S(2)}) async-start(), calls=%async_computation.11 | async-start | bytes 4866048 | tf_op jit(solution)/shard_map/all_gather | solution.py:133
  60.9 39.1 %copy-start.16 = (bf16[3072]{0:T(1024)(128)(2,1)}, bf16[3072]{0:T(1024)(128)(2,1)S(1)}, u32[]{:S(2)}) copy-start(bf16[3072]{0:T(1024)(128)(2,1)S(1)} %get-tuple-element.230) | copy-start | bytes 18436
  61.7 92.0 %copy-start.19 = (f32[768]{0:T(1024)}, f32[768]{0:T(1024)S(1)}, u32[]{:S(2)}) copy-start(f32[768]{0:T(1024)S(1)} %convert_element_type.124) | copy-start | bytes 9220
  109.7 44.0 %copy-start.11 = (f32[2,3,512,1]{2,1,3,0:T(4,128)}, f32[2,3,512,1]{2,1,3,0:T(4,128)S(1)}, u32[]{:S(2)}) copy-start(f32[2,3,512,1]{2,1,3,0:T(4,128)S(1)} %get-tuple-element.411) | copy-start | bytes 36868
  109.7 41.9 %copy-start.6 = (bf16[256,768]{1,0:T(8,128)(2,1)S(1)}, bf16[256,768]{1,0:T(8,128)(2,1)}, u32[]{:S(2)}) copy-start(bf16[256,768]{1,0:T(8,128)(2,1)} %param.21) | copy-start | bytes 1179652
  110.1 41.4 %copy-start.1 = (bf16[2,512,3,64]{1,0,3,2:T(2,128)(2,1)}, bf16[2,512,3,64]{1,0,3,2:T(2,128)(2,1)S(1)}, u32[]{:S(2)}) copy-start(bf16[2,512,3,64]{1,0,3,2:T(2,128)(2,1)S(1)} %copy.58) | copy-start | bytes 1179652
  111.1 40.5 %all-to-all-start = ((bf16[4,256,192]{1,2,0:T(8,128)(2,1)}), bf16[4,256,192]{1,2,0:T(8,128)(2,1)S(1)}, u32[]{:S(2)}, u32[]{:S(2)}) async-start(bf16[4,256,192]{1,2,0:T(8,128)(2,1)} %copy.59), calls=%async_computation | async-start | bytes 786432 | tf_op jit(solution)/shard_map/all_to_all | solution.py:172
  114.5 191.2 %all-gather.19.cloned.1.call-start = ((), (), s32[]{:S(2)}) async-start(), calls=%async_computation.12 | async-start | bytes 1966080 | tf_op jit(solution)/shard_map/all_gather | solution.py:198
  153.4 141.4 %copy-start.14 = (f32[256]{0:T(256)}, f32[256]{0:T(256)S(1)}, u32[]{:S(2)}) copy-start(f32[256]{0:T(256)S(1)} %broadcast_multiply_fusion.1) | copy-start | bytes 3076
  153.7 1.0 copy-start.26
  153.7 141.2 %copy-start.17 = (f32[256]{0:T(256)}, f32[256]{0:T(256)S(1)}, u32[]{:S(2)}) copy-start(f32[256]{0:T(256)S(1)} %fusion.89) | copy-start | bytes 3076
  154.7 140.4 %copy-start.7 = (bf16[256,768]{1,0:T(8,128)(2,1)S(1)}, bf16[256,768]{1,0:T(8,128)(2,1)}, u32[]{:S(2)}) copy-start(bf16[256,768]{1,0:T(8,128)(2,1)} %param.37) | copy-start | bytes 1179652
  154.7 140.4 %copy-start.13 = (f32[768]{0:T(1024)S(1)}, f32[768]{0:T(1024)}, u32[]{:S(2)}) copy-start(f32[768]{0:T(1024)} %convert_element_type.129) | copy-start | bytes 9220
  154.7 140.4 %copy-start.25 = (f32[256]{0:T(256)S(1)}, f32[256]{0:T(256)}, u32[]{:S(2)}) copy-start(f32[256]{0:T(256)} %dynamic-slice_convert_fusion) | copy-start | bytes 3076
  154.7 169.1 %all-gather.21.cloned.1.call-start = ((), (), s32[]{:S(2)}) async-start(), calls=%async_computation.13 | async-start | bytes 1966080 | tf_op jit(solution)/shard_map/all_gather | solution.py:199
  299.8 68.3 %reduce-scatter.10.cloned.1.call-start = ((), (), s32[]{:S(2)}) async-start(), calls=%async_computation.14 | async-start | bytes 1966080 | tf_op jit(solution)/shard_map/reduce_scatter | solution.py:222
  323.8 13.4 %copy-start.8 = (bf16[768,8,1,96]{0,3,2,1:T(8,128)(2,1)S(1)}, bf16[768,8,1,96]{0,3,2,1:T(8,128)(2,1)}, u32[]{:S(2)}) copy-start(bf16[768,8,1,96]{0,3,2,1:T(8,128)(2,1)} %constant_dynamic-slice_fusion.3) | copy-start | bytes 3538948
  336.0 1.2 copy-start.33
  337.2 30.9 %copy-start.15 = (f32[256]{0:T(256)S(1)}, f32[256]{0:T(256)}, u32[]{:S(2)}) copy-start(f32[256]{0:T(256)} %copy-done.14) | copy-start | bytes 3076
  337.2 30.9 %copy-start.18 = (f32[256]{0:T(256)S(1)}, f32[256]{0:T(256)}, u32[]{:S(2)}) copy-start(f32[256]{0:T(256)} %copy-done.17) | copy-start | bytes 3076
  339.7 30.4 %copy-start.27 = (f32[256]{0:T(256)S(1)}, f32[256]{0:T(256)}, u32[]{:S(2)}) copy-start(f32[256]{0:T(256)} %copy-done.26) | copy-start | bytes 3076
  339.8 33.8 %copy-start.2 = (bf16[2,512,3,64]{1,0,3,2:T(2,128)(2,1)S(1)}, bf16[2,512,3,64]{1,0,3,2:T(2,128)(2,1)}, u32[]{:S(2)}) copy-start(bf16[2,512,3,64]{1,0,3,2:T(2,128)(2,1)} %copy-done.1) | copy-start | bytes 1179652
  339.8 53.5 %all-gather.23.cloned.1.call-start = ((), (), s32[]{:S(2)}) async-start(), calls=%async_computation.15 | async-start | bytes 1966080 | tf_op jit(solution)/shard_map/all_gather | solution.py:234
  371.6 1.0 copy-start.3
  371.6 24.8 %copy-start.5 = (bf16[1024,768]{1,0:T(8,128)(2,1)S(1)}, bf16[1024,768]{1,0:T(8,128)(2,1)}, u32[]{:S(2)}) copy-start(bf16[1024,768]{1,0:T(8,128)(2,1)} %all-gather.21.cloned.1.call-done) | copy-start | bytes 4718596
  371.6 1.9 copy-start.29
  373.5 142.2 %reduce-scatter.18.cloned.1.call-start = ((), (), s32[]{:S(2)}) async-start(), calls=%async_computation.19 | async-start | bytes 884736
  396.4 135.6 %reduce-scatter.14.cloned.1.call-start = ((), (), s32[]{:S(2)}) async-start(), calls=%async_computation.17 | async-start | bytes 2654208 | tf_op jit(solution)/shard_map/reduce_scatter | solution.py:269
  402.2 202.2 %reduce-scatter.12.cloned.1.call-start = ((), (), s32[]{:S(2)}) async-start(), calls=%async_computation.16 | async-start | bytes 2654208 | tf_op jit(solution)/shard_map/reduce_scatter | solution.py:267
  402.2 5.2 copy-start
  407.1 2.5 copy-start.12
  407.2 267.2 %reduce-scatter.16.cloned.1.call-start = ((), (), s32[]{:S(2)}) async-start(), calls=%async_computation.18 | async-start | bytes 2211840
  413.0 1.3 copy-start.9
  414.4 1.0 copy-start.10
  418.7 1.3 copy-start.9
  420.0 1.0 copy-start.10
  421.1 2.9 copy-start.31
  429.8 7.6 %copy-start.32 = (u32[32]{0:T(128)S(1)}, u32[32]{0:T(128)}, u32[]{:S(2)}) copy-start(u32[32]{0:T(128)} %constant.268) | copy-start | bytes 388
  429.8 8.9 %copy-start.28 = (f32[768]{0:T(1024)S(1)}, f32[768]{0:T(1024)}, u32[]{:S(2)}) copy-start(f32[768]{0:T(1024)} %get-tuple-element.239) | copy-start | bytes 9220
  433.2 27.5 %all-to-all-start.1 = ((bf16[4,2,73728]{2,1,0:T(2,128)(2,1)}), bf16[4,2,73728]{2,1,0:T(2,128)(2,1)}, u32[]{:S(2)}, u32[]{:S(2)}) async-start(bf16[4,2,73728]{2,1,0:T(2,128)(2,1)} %reshape.407), calls=%async_computation.2 | async-start | bytes 2359296 | tf_op jit(solution)/shard_map/all_to_all | solution.py:249
  468.2 0.8 copy-start.20
  468.2 0.8 copy-start.21
  468.2 43.6 %copy-start.4 = (f32[256,768]{1,0:T(8,128)S(1)}, f32[256,768]{1,0:T(8,128)}, u32[]{:S(2)}) copy-start(f32[256,768]{1,0:T(8,128)} %copy-done.3) | copy-start | bytes 2359300
  468.3 43.6 %copy-start.30 = (f32[256]{0:T(256)S(1)}, f32[256]{0:T(256)}, u32[]{:S(2)}) copy-start(f32[256]{0:T(256)} %copy-done.29) | copy-start | bytes 3076
  (3 other events, 2.4 us)
Sparse Core Ops, SparseCore 0:
  9.6 22.9 all-gather.10
  35.4 60.3 all-gather.8
  98.7 52.8 all-gather.12
  154.3 62.5 all-gather.14
  219.7 62.4 all-gather.16
  284.1 18.4 all-gather.18
  304.1 19.6 all-gather.20
  339.9 28.1 reduce-scatter.9
  373.6 19.6 all-gather.22
  396.8 62.5 reduce-scatter.17
  463.4 68.4 reduce-scatter.13
  535.9 68.4 reduce-scatter.11
  608.4 65.8 reduce-scatter.15
where the time goes:
time: 690 us; the launch traced here: 681 us
  waiting for transfers between devices  415 us (60%)
  blocking collectives  102 us (15%)
  matrix products  69.3 us (10%)
  local copies, waits for them, and re-layouts  48.8 us (7%)
  other arithmetic  21.6 us (3%)
  between operations  15.7 us (2%)
  starting transfers between devices  8.88 us (1%)
    unnamed x3, blocking collectives  102 us
    unnamed x15, waiting for transfers between devices  73.2 us
    reduce_scatter x1, waiting for transfers between devices, local(): lax.psum_scatter(up_grad, 'batch', scatter_dimension=1, tiled=True)  72.4 us
    all_gather x1, waiting for transfers between devices, local(): lax.all_gather(down_weight, ('batch', 'head'), axis=0, tiled=True)  65.2 us
    all_gather x1, waiting for transfers between devices, local(): lax.all_gather(up_weight, ('batch', 'head'), axis=1, tiled=True)  62 us
    all_gather x1, waiting for transfers between devices, local(): lax.all_gather(proj_weight, ('batch', 'head'), axis=1, tiled=True)  35.6 us
    all_gather x1, waiting for transfers between devices, local(): lax.all_gather(qkv_weight, ('batch', 'head'), axis=1, tiled=True)  30.3 us
    reduce_scatter x1, waiting for transfers between devices, local(): lax.psum_scatter(jnp.einsum('rf,df->rd', up_cot, up_sel, preferred_elemen...  28.3 us
  transfers between devices with their start and end apart: 15, of which 10 were waited for; matrix products, arithmetic and copies ran while one was open for 17% of the time, Pallas kernels for 0%

commit v1 on v0

v1 whole, which is shorter than its diff:
```python
import jax
import jax.numpy as jnp
from jax import lax
from jax.experimental import pallas as pl
from jax.experimental.pallas import tpu as pltpu
from jax.sharding import PartitionSpec as P

D = 768
HEADS = 12
HEAD_DIM = 64
FF = 3072
BIG = 512
SMALL = 128
UNITS = 4
NORM_EPS = 1e-12
F32 = jnp.float32
BF16 = jnp.bfloat16

CORE = [(i, i ^ 1) for i in range(4)]
XPAIR = [(i, i ^ 2) for i in range(4)]
YPAIR = [(i, i ^ 1) for i in range(8)]
ZPAIR = [[(i, i ^ (2 * k)) for i in range(8)] for k in range(4)]


def core_swap(v):
    return lax.ppermute(v, "head", CORE)


def x_swap(v):
    return lax.ppermute(v, "head", XPAIR)


def y_swap(v):
    return lax.ppermute(v, "batch", YPAIR)


def z_swap(v, k):
    return lax.ppermute(v, "batch", ZPAIR[k])


def after(value, other):
    return lax.optimization_barrier((value, other))[0]


def nt(a, b, out=F32):
    return lax.dot_general(a, b, (((1,), (1,)), ((), ())), preferred_element_type=F32).astype(out)


def nn(a, b, out=F32):
    return lax.dot_general(a, b, (((1,), (0,)), ((), ())), preferred_element_type=F32).astype(out)


def tn(a, b, out=F32):
    return lax.dot_general(a, b, (((0,), (0,)), ((), ())), preferred_element_type=F32).astype(out)


def gather_plane(shard, direct):
    if not direct:
        whole = lax.all_gather(shard, "batch", axis=0)
        return [whole, x_swap(whole)]
    z = jnp.stack([shard] + [z_swap(shard, k) for k in (1, 2, 3)])
    x = x_swap(z)
    y = y_swap(z)
    return [z, x, y, x_swap(y[:2]), y_swap(x[2:])]


def scatter_plane(parts, direct):
    if not direct:
        total = parts[0].astype(F32) + x_swap(parts[1]).astype(F32)
        return lax.psum_scatter(total, "batch", scatter_dimension=0, tiled=False)
    g0, gx, gy, ga, gb = parts
    ra = x_swap(ga)
    rb = y_swap(gb)
    sy = jnp.concatenate([(gy[:2].astype(F32) + ra.astype(F32)).astype(BF16), gy[2:]])
    sx = jnp.concatenate([gx[:2], (gx[2:].astype(F32) + rb.astype(F32)).astype(BF16)])
    total = g0.astype(F32) + y_swap(sy).astype(F32) + x_swap(sx).astype(F32)
    return total


def finish_z(mine, others):
    return mine + sum(z_swap(others[k - 1].astype(BF16), k).astype(F32) for k in (1, 2, 3))


def order_kernel(rows_q, rows_p, place, *refs):
    sources, (wq, wp, sem) = refs[:10], refs[10:]
    z, y, x, c = place[0], place[1], place[2], place[3]
    copies = []
    for swapped in range(2):
        cc = c if swapped == 0 else 1 - c
        z0, xx, yy, xa, xb = sources[5 * swapped : 5 * swapped + 5]
        p = lax.rem(c + z, 2)
        for kx, ky, pair in ((0, 0, (z0, z0)), (1, 0, (xx, xx)), (0, 1, (yy, yy)), (1, 1, (xa, xb))):
            yi = y + ky - 2 * y * ky
            xi = x + kx - 2 * x * kx
            j = yi * 4 + xi * 2 + cc
            for i in range(2):
                src = pair[i]
                spot = p if pair[0] is not pair[1] else p + 2 * i
                zh = lax.div(z, 2)
                g = zh + i - 2 * zh * i
                copies.append(
                    pltpu.make_async_copy(src.at[spot, pl.ds(0, rows_q)], wq.at[g, j], sem)
                )
            for kz in range(4):
                src = pair[kz // 2]
                spot = kz if pair[0] is pair[1] else kz - 2 * (kz // 2)
                zl, zh = lax.rem(z, 2), lax.div(z, 2)
                k0, k1 = kz % 2, kz // 2
                zi = (zl + k0 - 2 * zl * k0) + 2 * (zh + k1 - 2 * zh * k1)
                copies.append(
                    pltpu.make_async_copy(
                        src.at[spot, pl.ds(rows_q, rows_p)], wp.at[zi * 8 + j], sem
                    )
                )
    for copy in copies:
        copy.start()
    for copy in copies:
        copy.wait()


def order_weights(own, swapped, place, rows_q, rows_p):
    import functools

    return pl.pallas_call(
        functools.partial(order_kernel, rows_q, rows_p),
        out_shape=(
            jax.ShapeDtypeStruct((2, 8, rows_q, D), BF16),
            jax.ShapeDtypeStruct((32, rows_p, D), BF16),
        ),
        grid_spec=pltpu.PrefetchScalarGridSpec(
            num_scalar_prefetch=1,
            grid=(1,),
            in_specs=[pl.BlockSpec(memory_space=pl.ANY)] * 10,
            out_specs=[pl.BlockSpec(memory_space=pl.ANY)] * 2,
            scratch_shapes=[pltpu.SemaphoreType.DMA],
        ),
    )(place, *own, *swapped)


def norm_parts(values):
    center = values - jnp.mean(values, -1, keepdims=True)
    spread = jnp.mean(center * center, -1, keepdims=True)
    scale = lax.rsqrt(spread + NORM_EPS)
    return center * scale, scale


def norm_back(cot, normal, scale, gain):
    w = cot * gain
    return scale * (
        w - jnp.mean(w, -1, keepdims=True) - normal * jnp.mean(w * normal, -1, keepdims=True)
    )


def masks(bucket, lengths, chip_half, c):
    units = jnp.arange(UNITS, dtype=jnp.int32)
    long_live = jnp.clip(lengths[0] - SMALL * units, 0, SMALL)
    unit_live = jnp.where(bucket == 1, long_live, lengths)
    places = jnp.arange(BIG, dtype=jnp.int32)
    unit_of = places // SMALL
    live = (places - unit_of * SMALL) < jnp.repeat(unit_live, SMALL)
    segment = jnp.where(bucket == 1, 0, unit_of)
    live = jnp.where(c == 0, live, jnp.roll(live, BIG // 2))
    segment = jnp.where(c == 0, segment, jnp.roll(segment, BIG // 2))
    return live, segment


def local(
    inputs,
    bucket,
    lengths,
    qkv_weight,
    query_bias,
    value_bias,
    proj_weight,
    proj_bias,
    first_gain,
    first_shift,
    up_weight,
    up_bias,
    down_weight,
    down_bias,
    second_gain,
    second_shift,
    cotangent,
):
    head_count = lax.axis_size("head")
    batch_count = lax.axis_size("batch")
    devices = head_count * batch_count
    direct = batch_count == 8
    b = lax.axis_index("batch")
    h = lax.axis_index("head")
    me = b * head_count + h
    x, c = h // 2, h % 2
    z, y = b // 2, b % 2
    rows = inputs.shape[0]
    wq, wp, wf = 3 * D // devices, D // devices, FF // devices

    vectors = jnp.stack(
        [
            query_bias,
            value_bias,
            proj_bias,
            first_gain,
            first_shift,
            down_bias,
            second_gain,
            second_shift,
        ]
    )
    small = lax.dynamic_update_slice(jnp.zeros((8, D), BF16), vectors, (0, me * wp))
    proj_t = proj_weight.T.reshape(wp, 2, 2, 192).transpose(0, 2, 1, 3).reshape(wp, D)
    a_shard = jnp.concatenate([qkv_weight.T, proj_t, small])
    bias_row = jnp.pad(up_bias[None, :], ((0, 7), (0, D - wf)))
    u_shard = jnp.concatenate([up_weight.T, bias_row])

    other_in = core_swap(inputs)
    group_in = jnp.concatenate([inputs, other_in])

    if direct:
        a_own = gather_plane(a_shard, direct)
        u_shard = after(u_shard, a_own[0])
        u_all = gather_plane(u_shard, direct)
        d_shard = after(down_weight, u_all[0])
        d_all = gather_plane(d_shard, direct)
        a_swapped = [core_swap(v) for v in a_own]
        place = jnp.stack([z, y, x, c]).astype(jnp.int32)
        qkv_w, proj_w = order_weights(a_own, a_swapped, place, wq, wp)
        qkv_w = qkv_w.reshape(2 * 576, D)
        proj_w = proj_w.reshape(D, D)
        small_all = sum(jnp.sum(v[:, wq + wp :].astype(F32), 0) for v in a_own + a_swapped)
    else:
        a_all = lax.all_gather(a_shard, ("batch", "head"), axis=0)
        qkv_all = a_all[:, :wq].reshape(2, 2, 576, D)
        qkv_w = lax.dynamic_index_in_dim(qkv_all, c, 1, keepdims=False).reshape(2 * 576, D)
        proj_w = a_all[:, wq : wq + wp].reshape(D, D)
        small_all = jnp.sum(a_all[:, wq + wp :].astype(F32), 0)
        u_all = gather_plane(u_shard, direct)
        d_all = gather_plane(down_weight, direct)
    qbias, vbias, pbias, fgain, fshift, dbias, sgain, sshift = [small_all[i] for i in range(8)]

    live, segment = masks(
        lax.dynamic_index_in_dim(bucket, x, 0, keepdims=False),
        lax.dynamic_index_in_dim(lengths, x, 0, keepdims=False),
        x,
        c,
    )
    own_live = live[:rows]

    q_own = lax.dynamic_index_in_dim(qbias.reshape(2, 2, 192), c, 1, keepdims=False)
    v_own = lax.dynamic_index_in_dim(vbias.reshape(2, 2, 192), c, 1, keepdims=False)
    bias = jnp.stack(
        [q_own.reshape(6, HEAD_DIM), jnp.zeros((6, HEAD_DIM), F32), v_own.reshape(6, HEAD_DIM)], 1
    ).reshape(-1)
    by_heads = (nt(group_in, qkv_w) + bias).astype(BF16).reshape(2 * rows, 6, 3, HEAD_DIM)
    query, keys, values = by_heads[:, :, 0], by_heads[:, :, 1], by_heads[:, :, 2]
    allowed = (segment[:, None] == segment[None, :]) & live[None, :]
    scale = HEAD_DIM ** (-0.5)
    scores = jnp.einsum("qhd,khd->hqk", query, keys, preferred_element_type=F32) * scale
    scores = jnp.where(allowed[None], scores, -1e30)
    highest = jnp.max(scores, -1, keepdims=True)
    exp_vals = jnp.exp(scores - highest)
    probs = exp_vals / jnp.sum(exp_vals, -1, keepdims=True)
    probs_low = probs.astype(BF16)
    context = jnp.einsum("hqk,khd->qhd", probs_low, values, preferred_element_type=F32)
    context = context.astype(BF16).reshape(2 * rows, 384)
    ctx_in = core_swap(context[rows:])
    ctx_own = context[:rows]
    context_tok = jnp.where(
        c == 0,
        jnp.concatenate([ctx_own, ctx_in], 1),
        jnp.concatenate([ctx_in, ctx_own], 1),
    )
    attn = nt(context_tok, proj_w) + pbias
    first_n, first_r = norm_parts(inputs.astype(F32) + attn)
    first = first_n * fgain + fshift
    first_low = first.astype(BF16)
    first_group = jnp.concatenate([first_low, core_swap(first_low)])

    down_part = 0.0
    kept = []
    for u, d in zip(u_all, d_all):
        n = u.shape[0]
        up_w = u[:, :wf].reshape(n * wf, D)
        up_b = u[:, wf, :wf].reshape(n * wf).astype(F32)
        dn_w = d.reshape(n * wf, D)
        up_val = nt(first_group, up_w) + up_b
        phi = 0.5 * (1.0 + lax.erf(up_val * (2.0**-0.5)))
        hidden = (up_val * phi).astype(BF16)
        slope = (phi + up_val * jnp.exp(-0.5 * up_val * up_val) * 0.3989422804014327).astype(BF16)
        down_part = down_part + nn(hidden, dn_w)
        kept.append((up_w, dn_w, hidden, slope))
    down = down_part[:rows] + core_swap(down_part[rows:]) + dbias
    second_n, second_r = norm_parts(first + down)
    layer_out = (second_n * sgain + sshift).astype(BF16)

    out_cot = cotangent.astype(F32) * own_live[:, None].astype(F32)
    sum_two_cot = norm_back(out_cot, second_n, second_r, sgain)
    sgain_grad = jnp.sum(out_cot * second_n, 0)
    sshift_grad = jnp.sum(out_cot, 0)
    down_cot = sum_two_cot.astype(BF16)
    dbias_grad = jnp.sum(down_cot.astype(F32), 0)
    down_group = jnp.concatenate([down_cot, core_swap(down_cot)])
    ffn_part = 0.0
    up_parts, down_parts, ubias_parts = [], [], []
    for up_w, dn_w, hidden, slope in kept:
        n = up_w.shape[0] // wf
        hidden_cot = nt(down_group, dn_w)
        up_cot = (hidden_cot * slope.astype(F32)).astype(BF16)
        down_parts.append(tn(hidden, down_group, BF16).reshape(n, wf, D))
        up_parts.append(tn(up_cot, first_group, BF16).reshape(n, wf, D))
        ubias_parts.append(jnp.sum(up_cot.astype(F32), 0).reshape(n, wf))
        ffn_part = ffn_part + nn(up_cot, up_w)
    first_cot = sum_two_cot + ffn_part[:rows] + core_swap(ffn_part[rows:])
    sum_one_cot = norm_back(first_cot, first_n, first_r, fgain)
    fgain_grad = jnp.sum(first_cot * first_n, 0)
    fshift_grad = jnp.sum(first_cot, 0)
    attn_cot = sum_one_cot.astype(BF16)
    pbias_grad = jnp.sum(attn_cot.astype(F32), 0)
    attn_group = jnp.concatenate([attn_cot, core_swap(attn_cot)])
    proj_own = lax.dynamic_slice_in_dim(proj_w, c * 384, 384, 1)
    ctx_cot = nn(attn_group, proj_own, BF16).reshape(2 * rows, 6, HEAD_DIM)
    value_cot = jnp.einsum("hqk,qhd->khd", probs_low, ctx_cot, preferred_element_type=F32)
    prob_cot = jnp.einsum("qhd,khd->hqk", ctx_cot, values, preferred_element_type=F32)
    score_cot = (probs * (prob_cot - jnp.sum(probs * prob_cot, -1, keepdims=True))).astype(BF16)
    query_cot = jnp.einsum("hqk,khd->qhd", score_cot, keys, preferred_element_type=F32) * scale
    keys_cot = jnp.einsum("hqk,qhd->khd", score_cot, query, preferred_element_type=F32) * scale
    qkv_cot = jnp.stack([query_cot, keys_cot, value_cot], axis=2).astype(BF16)
    head_sums = jnp.sum(qkv_cot.astype(F32), 0)
    qkv_heads = qkv_cot.reshape(2 * rows, 2 * 576)
    in_part = nn(qkv_heads, qkv_w)
    inputs_grad = (sum_one_cot + in_part[:rows] + core_swap(in_part[rows:])).astype(BF16)

    a_grads = jnp.stack(
        [
            jnp.concatenate(
                [
                    tn(group_in, qkv_heads[:, 576 * g : 576 * g + 576], BF16),
                    tn(attn_group, context[:, 192 * g : 192 * g + 192], BF16),
                ],
                1,
            )
            for g in range(2)
        ]
    )
    wb = D // batch_count
    if direct:
        a_grads = a_grads.reshape(2, 4, 2, wb, D)

        def pick(xi, yi):
            return lax.dynamic_slice(a_grads, (xi, 0, yi, 0, 0), (1, 4, 1, wb, D)).reshape(4, wb, D)

        diag = pick(1 - x, 1 - y)
        a_total = scatter_plane(
            [pick(x, y), pick(1 - x, y), pick(x, 1 - y), diag[:2], diag[2:]], direct
        )
        a_mine = finish_z(
            lax.dynamic_index_in_dim(a_total, z, 0, keepdims=False),
            [lax.dynamic_index_in_dim(a_total, z ^ k, 0, keepdims=False) for k in (1, 2, 3)],
        )
        d_total = scatter_plane(down_parts, direct)
        d_mine = finish_z(d_total[0], d_total[1:])
        u_total = scatter_plane(up_parts, direct)
        u_mine = finish_z(u_total[0], u_total[1:])
    else:
        a_grads = a_grads.reshape(2, batch_count, wb, D)
        a_mine = scatter_plane(
            [
                lax.dynamic_index_in_dim(a_grads, x, 0, keepdims=False),
                lax.dynamic_index_in_dim(a_grads, 1 - x, 0, keepdims=False),
            ],
            direct,
        )
        d_mine = scatter_plane(down_parts, direct)
        u_mine = scatter_plane(up_parts, direct)
    qkv_grad = a_mine[:, :576]
    proj_grad = a_mine[:, 576:].T
    up_grad = u_mine.T
    down_grad = d_mine

    def place_heads(v):
        v = v.reshape(2, 1, 192)
        keep = (jnp.arange(2) == c).astype(F32)[None, :, None]
        return (v * keep).reshape(D)

    sums = jnp.stack(
        [
            place_heads(head_sums[:, 0]),
            place_heads(head_sums[:, 2]),
            pbias_grad,
            fgain_grad,
            fshift_grad,
            dbias_grad,
            sgain_grad,
            sshift_grad,
        ]
    )
    sums = sums.reshape(8, devices, wp).transpose(1, 0, 2).reshape(devices, 8 * wp)
    ubias = jnp.concatenate(ubias_parts)
    k = jnp.arange(batch_count * 2)
    if direct:
        kz = jnp.array([0, 1, 2, 3] * 3 + [0, 1, 2, 3])
        ky = jnp.array([0] * 8 + [1] * 8)
        kx = jnp.array([0] * 4 + [1] * 4 + [0] * 4 + [1] * 4)
        owner = (z ^ kz) * 8 + (y ^ ky) * 4 + (x ^ kx) * 2 + c
    else:
        owner = (k % batch_count) * 4 + (x ^ (k // batch_count)) * 2 + c
    spread = (owner[None, :] == jnp.arange(devices)[:, None]).astype(F32)
    ubias = lax.dot_general(
        spread, ubias, (((1,), (0,)), ((), ())), precision=lax.Precision.HIGHEST
    )
    packed = jnp.concatenate([sums, ubias], 1)
    packed = lax.all_to_all(packed, ("batch", "head"), split_axis=0, concat_axis=0, tiled=True)
    packed = jnp.sum(packed, 0)
    vecs = [packed[i * wp : (i + 1) * wp] for i in range(8)]
    return (
        layer_out,
        inputs_grad,
        qkv_grad,
        vecs[0],
        vecs[1],
        proj_grad,
        vecs[2],
        vecs[3],
        vecs[4],
        up_grad,
        packed[8 * wp :],
        down_grad,
        vecs[5],
        vecs[6],
        vecs[7],
    )


def solution(mesh):
    both = ("batch", "head")
    in_specs = (
        P(both, None),
        P("batch"),
        P("batch", None),
        P(None, both),
        P(both),
        P(both),
        P(None, both),
        P(both),
        P(both),
        P(both),
        P(None, both),
        P(both),
        P(both, None),
        P(both),
        P(both),
        P(both),
        P(both, None),
    )
    out_specs = (
        P(both, None),
        P(both, None),
        P("batch", "head"),
        P(both),
        P(both),
        P("head", "batch"),
        P(both),
        P(both),
        P(both),
        P(None, both),
        P(both),
        P(both, None),
        P(both),
        P(both),
        P(both),
    )
    return jax.shard_map(local, mesh=mesh, in_specs=in_specs, out_specs=out_specs, check_vma=False)
```

time: 690 us -> 411 us (0.60)
  waiting for transfers between devices: 415 us -> 60.6 us
  blocking collectives: 102 us -> 0 us
  Pallas kernels: 0 us -> 91.1 us
  starting transfers between devices: 8.88 us -> 55.5 us
  other arithmetic: 21.6 us -> 46.1 us
  local copies, waits for them, and re-layouts: 48.8 us -> 68.9 us
  between operations: 15.7 us -> 3.33 us
  matrix products: 69.3 us -> 78.8 us
    all_gather x8 -> x0, waiting for transfers between devices: 226 us -> none  [the longest x1 65.2 us: local(): lax.all_gather(down_weight, ('batch', 'head'), axis=0, tiled=True)]
    reduce_scatter x3 -> x0, waiting for transfers between devices: 115 us -> none  [the longest x1 72.4 us: local(): lax.psum_scatter(up_grad, 'batch', scatter_dimension=1, tiled=True)]
    unnamed x3 -> x0, blocking collectives: 102 us -> none
    pallas_call x0 -> x1, Pallas kernels: none -> 91.1 us  [order_weights(): pl.pallas_call(functools.partial(order_kernel, rows_q, rows_p), out_shape...]
    unnamed x15 -> x0, waiting for transfers between devices: 73.2 us -> none
    ppermute x0 -> x55, waiting for transfers between devices: none -> 55.5 us  [the longest x18 31.4 us: z_swap(): return lax.ppermute(v, 'batch', ZPAIR[k])]
    ppermute x0 -> x55, starting transfers between devices: none -> 50.1 us  [the longest x18 23.7 us: z_swap(): return lax.ppermute(v, 'batch', ZPAIR[k])]
    slice x1 -> x29, local copies, waits for them, and re-layouts: 0.79 us -> 22.1 us  [the longest x6 6.86 us: gather_plane(): return [z, x, y, x_swap(y[:2]), y_swap(x[2:])]]
  transfers between devices with their start and end apart: 15 -> 56, of which waited for: 10 -> 15; matrix products, arithmetic and copies ran while one was open for 17% -> 40% of each run, Pallas kernels for 0% -> 23%
where the time goes in v1:
time: 411 us; the launch traced here: 404 us
  Pallas kernels  91.1 us (22%)
  matrix products  78.8 us (19%)
  local copies, waits for them, and re-layouts  68.9 us (17%)
  waiting for transfers between devices  60.6 us (15%)
  starting transfers between devices  55.5 us (14%)
  other arithmetic  46.1 us (11%)
    pallas_call x1, Pallas kernels, order_weights(): pl.pallas_call(functools.partial(order_kernel, rows_q, rows_p), out_shape...  91.1 us
    ppermute x18, waiting for transfers between devices, z_swap(): return lax.ppermute(v, 'batch', ZPAIR[k])  31.4 us
    dot_general x12, matrix products, nt(): lax.dot_general(a, b, (((1,), (1,)), ((), ())), preferred_element_type=F32)  27 us
    ppermute x18, starting transfers between devices, z_swap(): return lax.ppermute(v, 'batch', ZPAIR[k])  23.7 us
    dot_general x14, matrix products, tn(): lax.dot_general(a, b, (((0,), (0,)), ((), ())), preferred_element_type=F32)  22.8 us
    unnamed x217, local copies, waits for them, and re-layouts  17 us
    ppermute x12, waiting for transfers between devices, y_swap(): return lax.ppermute(v, 'batch', YPAIR)  15.9 us
    dot_general x12, matrix products, nn(): lax.dot_general(a, b, (((1,), (0,)), ((), ())), preferred_element_type=F32)  13.9 us
  transfers between devices with their start and end apart: 56, of which 15 were waited for; matrix products, arithmetic and copies ran while one was open for 40% of the time, Pallas kernels for 23%

profile of v1, /device:TPU:0, one launch (start us, length us, event | category | flops | bytes accessed | tf_op | source)
XLA Modules:
  0.0 404.5 jit_solution(14191128058453206030)
XLA Ops:
  3.6 5.2 %collective-permute-start.3 = (bf16[104,768]{1,0:T(8,128)(2,1)S(1)}, bf16[104,768]{1,0:T(8,128)(2,1)S(1)}, u32[]{:S(2)}, u32[]{:S(2)}) collective-permute-start(bf16[104,768]{1,0:T(8,128)(2,1)S(1)} %get-tuple-element.139), channel_id=1, source_target_pairs={{0,24},{4,28},{8,16},{12,20},{16,8},{20,12},{24,0},{28,4},{1,25},{... | collective-permute-start | bytes 479240 | tf_op jit(solution)/shard_map/ppermute | solution.py:38
  14.0 8.4 %collective-permute-done.2 = bf16[104,768]{1,0:T(8,128)(2,1)S(1)} collective-permute-done((bf16[104,768]{1,0:T(8,128)(2,1)S(1)}, bf16[104,768]{1,0:T(8,128)(2,1)S(1)}, u32[]{:S(2)}, u32[]{:S(2)}) %collective-permute-start.2) | collective-permute-done | bytes 159776 | tf_op jit(solution)/shard_map/ppermute | solution.py:38
  25.6 2.5 collective-permute-start.17
  29.8 4.0 collective-permute-done.17
  33.8 6.4 %collective-permute-done.16 = bf16[104,768]{1,0:T(8,128)(2,1)S(1)} collective-permute-done((bf16[104,768]{1,0:T(8,128)(2,1)S(1)}, bf16[104,768]{1,0:T(8,128)(2,1)S(1)}, u32[]{:S(2)}, u32[]{:S(2)}) %collective-permute-start.16) | collective-permute-done | bytes 159776 | tf_op jit(solution)/shard_map/ppermute | solution.py:38
  41.4 4.1 %collective-permute-done.15 = bf16[104,768]{1,0:T(8,128)(2,1)S(1)} collective-permute-done((bf16[104,768]{1,0:T(8,128)(2,1)S(1)}, bf16[104,768]{1,0:T(8,128)(2,1)S(1)}, u32[]{:S(2)}, u32[]{:S(2)}) %collective-permute-start.15) | collective-permute-done | bytes 159776 | tf_op jit(solution)/shard_map/ppermute | solution.py:38
  47.2 1.9 constant_dynamic-update-slice_fusion
  52.9 6.8 %collective-permute-done.7.refs_4_ = bf16[2,104,768]{2,1,0:T(8,128)(2,1)S(1)} collective-permute-done((bf16[2,104,768]{2,1,0:T(8,128)(2,1)S(1)}, bf16[2,104,768]{2,1,0:T(8,128)(2,1)S(1)}, u32[]{:S(2)}, u32[]{:S(2)}) %collective-permute-start.7) | collective-permute-done | bytes 319520 | tf_op jit(solution)/shard_map/ppermute | solution.py:34
  61.1 1.9 collective-permute-start.20
  63.2 2.5 collective-permute-start.18
  67.6 91.1 %shard_map.307 = (bf16[2,8,72,768]{3,2,1,0:T(8,128)(2,1)}, bf16[32,24,768]{2,1,0:T(8,128)(2,1)}) custom-call(s32[4]{0:T(128)} %pad_add_fusion.place, bf16[4,104,768]{2,1,0:T(8,128)(2,1)} %copy-done.8, bf16[4,104,768]{2,1,0:T(8,128)(2,1)} %copy-done.17, bf16[4,104,768]{2,1,0:T(8,128)(2,1)} %copy-done.18, bf16[2,104,768]{2,1,0:T(8,128)(2,1)} %copy-done.58, ...), custom_call_target="tpu_custom_call" | custom-call | tf_op jit(solution)/shard_map/pallas_call | solution.py:124
  158.7 2.9 fusion.5
  162.5 6.2 %fusion.139 = (f32[6,512]{1,0:T(8,128)S(1)}, f32[6,512,512]{1,2,0:T(8,128)}) fusion(pred[512,512]{0,1:T(8,128)(4,1)} %compare_and_fusion, bf16[512,6,3,64]{0,3,2,1:T(8,128)(2,1)S(1)} %bitcast.266), kind=kOutput, calls=%fused_computation.325 | convolution fusion | flops 207618560 | bytes 7352320 | tf_op jit(solution)/shard_map/sub | solution.py:261
  168.7 3.5 fusion.19
  184.6 1.9 slice.451
  187.7 2.8 collective-permute-done.24
  195.9 2.2 collective-permute-done.25
  204.4 2.6 multiply_convert_fusion.1
  208.8 2.5 multiply_convert_fusion.3
  211.8 2.5 multiply_convert_fusion.2
  227.5 2.5 convert_reduce_fusion.7
  231.5 2.9 convert_reduce_fusion.1
  235.6 2.4 convert_reduce_fusion.3
  239.3 2.6 convert_reduce_fusion.2
  243.1 2.4 convert_reduce_fusion.6
  256.7 2.0 convolution_convert_fusion.13
  262.6 2.1 convolution_convert_fusion.14
  268.6 2.2 convolution_convert_fusion.11
  273.8 2.2 convolution_convert_fusion.12
  276.6 2.6 concatenate.90
  279.2 2.6 convolution_convert_fusion.7
  283.3 2.5 convolution_convert_fusion.4
  297.8 3.2 multiply_reduce_fusion.2
  304.3 3.3 collective-permute-done.42
  309.3 2.0 collective-permute-start.47
  311.3 3.7 collective-permute-done.51
  315.0 3.0 collective-permute-done.49
  318.0 2.6 fusion.122
  323.3 2.5 collective-permute-start.52
  345.1 2.2 collective-permute-start.34
  363.1 2.8 fusion.148
  371.6 5.5 %all-to-all-start = ((f32[32,1,288]{2,1,0:T(1,128)}), f32[32,1,288]{2,1,0:T(1,128)S(1)}, u32[]{:S(2)}, u32[]{:S(2)}) async-start(f32[32,1,288]{2,1,0:T(1,128)} %copy.102), calls=%async_computation | async-start | bytes 98304 | tf_op jit(solution)/shard_map/all_to_all | solution.py:412
  377.4 1.9 fusion.86
  379.3 5.1 %all-to-all-done = f32[32,1,288]{2,1,0:T(1,128)S(1)} async-done(((f32[32,1,288]{2,1,0:T(1,128)}), f32[32,1,288]{2,1,0:T(1,128)S(1)}, u32[]{:S(2)}, u32[]{:S(2)}) %all-to-all-start) | async-done | bytes 36896 | tf_op jit(solution)/shard_map/all_to_all | solution.py:412
  389.6 2.3 collective-permute-start.38
  391.9 2.0 fusion.43
  394.0 2.2 collective-permute-done.40
  396.2 6.2 %collective-permute-done.39 = bf16[96,768]{1,0:T(8,128)(2,1)S(1)} collective-permute-done((bf16[96,768]{1,0:T(8,128)(2,1)S(1)}, bf16[96,768]{1,0:T(8,128)(2,1)S(1)}, u32[]{:S(2)}, u32[]{:S(2)}) %collective-permute-start.39) | collective-permute-done | bytes 147488 | tf_op jit(solution)/shard_map/ppermute | solution.py:38
  (481 shorter events, 159.8 us)
Async XLA Ops:
  3.6 10.3 %collective-permute-start.3 = (bf16[104,768]{1,0:T(8,128)(2,1)S(1)}, bf16[104,768]{1,0:T(8,128)(2,1)S(1)}, u32[]{:S(2)}, u32[]{:S(2)}) collective-permute-start(bf16[104,768]{1,0:T(8,128)(2,1)S(1)} %get-tuple-element.139), channel_id=1, source_target_pairs={{0,24},{4,28},{8,16},{12,20},{16,8},{20,12},{24,0},{28,4},{1,25},{... | collective-permute-start | bytes 479240 | tf_op jit(solution)/shard_map/ppermute | solution.py:38
  8.8 13.5 %collective-permute-start.2 = (bf16[104,768]{1,0:T(8,128)(2,1)S(1)}, bf16[104,768]{1,0:T(8,128)(2,1)S(1)}, u32[]{:S(2)}, u32[]{:S(2)}) collective-permute-start(bf16[104,768]{1,0:T(8,128)(2,1)S(1)} %get-tuple-element.139), channel_id=1, source_target_pairs={{0,16},{4,20},{8,24},{12,28},{16,0},{20,4},{24,8},{28,12},{1,17},{... | collective-permute-start | bytes 479240 | tf_op jit(solution)/shard_map/ppermute | solution.py:38
  8.8 13.5 %collective-permute-start.1 = (bf16[104,768]{1,0:T(8,128)(2,1)S(1)}, bf16[104,768]{1,0:T(8,128)(2,1)S(1)}, u32[]{:S(2)}, u32[]{:S(2)}) collective-permute-start(bf16[104,768]{1,0:T(8,128)(2,1)S(1)} %get-tuple-element.139), channel_id=1, source_target_pairs={{0,8},{4,12},{8,0},{12,4},{16,24},{20,28},{24,16},{28,20},{1,9},{5... | collective-permute-start | bytes 479240 | tf_op jit(solution)/shard_map/ppermute | solution.py:38
  9.5 37.7 %collective-permute-start = (bf16[256,768]{1,0:T(8,128)(2,1)}, bf16[256,768]{1,0:T(8,128)(2,1)}, u32[]{:S(2)}, u32[]{:S(2)}) collective-permute-start(bf16[256,768]{1,0:T(8,128)(2,1)} %param.20), channel_id=1, source_target_pairs={{0,1},{1,0},{2,3},{3,2},{4,5},{5,4},{6,7},{7,6},{8,9},{9,8},{10,11... | collective-permute-start | bytes 1179656 | tf_op jit(solution)/shard_map/ppermute | solution.py:26
  22.5 26.7 %collective-permute-start.4 = (bf16[4,104,768]{2,1,0:T(8,128)(2,1)S(1)}, bf16[4,104,768]{2,1,0:T(8,128)(2,1)S(1)}, u32[]{:S(2)}, u32[]{:S(2)}) collective-permute-start(bf16[4,104,768]{2,1,0:T(8,128)(2,1)S(1)} %pad_maximum_fusion.5.refs_0_), channel_id=1, source_target_pairs={{0,2},{1,3},{2,0},{3,1},{4,6},{5,7},{6,4},{7,5},{8,10},{9,11},{10,... | collective-permute-start | bytes 1916936 | tf_op jit(solution)/shard_map/ppermute | solution.py:30
  24.0 23.1 %collective-permute-start.5 = (bf16[4,104,768]{2,1,0:T(8,128)(2,1)S(1)}, bf16[4,104,768]{2,1,0:T(8,128)(2,1)S(1)}, u32[]{:S(2)}, u32[]{:S(2)}) collective-permute-start(bf16[4,104,768]{2,1,0:T(8,128)(2,1)S(1)} %pad_maximum_fusion.5.refs_0_), channel_id=1, source_target_pairs={{0,4},{4,0},{8,12},{12,8},{16,20},{20,16},{24,28},{28,24},{1,5},{5... | collective-permute-start | bytes 1916936 | tf_op jit(solution)/shard_map/ppermute | solution.py:34
  28.0 12.2 %collective-permute-start.16 = (bf16[104,768]{1,0:T(8,128)(2,1)S(1)}, bf16[104,768]{1,0:T(8,128)(2,1)S(1)}, u32[]{:S(2)}, u32[]{:S(2)}) collective-permute-start(bf16[104,768]{1,0:T(8,128)(2,1)S(1)} %fusion.91), channel_id=1, source_target_pairs={{0,16},{4,20},{8,24},{12,28},{16,0},{20,4},{24,8},{28,12},{1,17},{... | collective-permute-start | bytes 479240 | tf_op jit(solution)/shard_map/ppermute | solution.py:38
  33.8 16.7 %collective-permute-start.8 = (bf16[4,104,768]{2,1,0:T(8,128)(2,1)S(1)}, bf16[4,104,768]{2,1,0:T(8,128)(2,1)}, u32[]{:S(2)}, u32[]{:S(2)}) collective-permute-start(bf16[4,104,768]{2,1,0:T(8,128)(2,1)S(1)} %pad_maximum_fusion.5.refs_0_), channel_id=1, source_target_pairs={{0,1},{1,0},{2,3},{3,2},{4,5},{5,4},{6,7},{7,6},{8,9},{9,8},{10,11... | collective-permute-start | bytes 1916936 | tf_op jit(solution)/shard_map/ppermute | solution.py:26
  47.2 13.1 %collective-permute-start.10 = (bf16[4,104,768]{2,1,0:T(8,128)(2,1)S(1)}, bf16[4,104,768]{2,1,0:T(8,128)(2,1)S(1)}, u32[]{:S(2)}, u32[]{:S(2)}) collective-permute-start(bf16[4,104,768]{2,1,0:T(8,128)(2,1)S(1)} %collective-permute-done.5.refs_2_), channel_id=1, source_target_pairs={{0,1},{1,0},{2,3},{3,2},{4,5},{5,4},{6,7},{7,6},{8,9},{9,8},{10,11... | collective-permute-start | bytes 1916936 | tf_op jit(solution)/shard_map/ppermute | solution.py:26
  49.2 10.4 %collective-permute-start.7 = (bf16[2,104,768]{2,1,0:T(8,128)(2,1)S(1)}, bf16[2,104,768]{2,1,0:T(8,128)(2,1)S(1)}, u32[]{:S(2)}, u32[]{:S(2)}) collective-permute-start(bf16[2,104,768]{2,1,0:T(8,128)(2,1)S(1)} %slice.426), channel_id=1, source_target_pairs={{0,4},{4,0},{8,12},{12,8},{16,20},{20,16},{24,28},{28,24},{1,5},{5... | collective-permute-start | bytes 958472 | tf_op jit(solution)/shard_map/ppermute | solution.py:34
  49.8 10.4 %collective-permute-start.6 = (bf16[2,104,768]{2,1,0:T(8,128)(2,1)S(1)}, bf16[2,104,768]{2,1,0:T(8,128)(2,1)S(1)}, u32[]{:S(2)}, u32[]{:S(2)}) collective-permute-start(bf16[2,104,768]{2,1,0:T(8,128)(2,1)S(1)} %slice.425), channel_id=1, source_target_pairs={{0,2},{1,3},{2,0},{3,1},{4,6},{5,7},{6,4},{7,5},{8,10},{9,11},{10,... | collective-permute-start | bytes 958472 | tf_op jit(solution)/shard_map/ppermute | solution.py:30
  50.4 10.5 %collective-permute-start.9 = (bf16[4,104,768]{2,1,0:T(8,128)(2,1)S(1)}, bf16[4,104,768]{2,1,0:T(8,128)(2,1)S(1)}, u32[]{:S(2)}, u32[]{:S(2)}) collective-permute-start(bf16[4,104,768]{2,1,0:T(8,128)(2,1)S(1)} %collective-permute-done.4.refs_1_), channel_id=1, source_target_pairs={{0,1},{1,0},{2,3},{3,2},{4,5},{5,4},{6,7},{7,6},{8,9},{9,8},{10,11... | collective-permute-start | bytes 1916936 | tf_op jit(solution)/shard_map/ppermute | solution.py:26
  50.5 125.7 %collective-permute-start.23 = (bf16[4,104,768]{2,1,0:T(8,128)(2,1)S(1)}, bf16[4,104,768]{2,1,0:T(8,128)(2,1)}, u32[]{:S(2)}, u32[]{:S(2)}) collective-permute-start(bf16[4,104,768]{2,1,0:T(8,128)(2,1)S(1)} %pad_maximum_fusion.6), channel_id=1, source_target_pairs={{0,4},{4,0},{8,12},{12,8},{16,20},{20,16},{24,28},{28,24},{1,5},{5... | collective-permute-start | bytes 1916936 | tf_op jit(solution)/shard_map/ppermute | solution.py:34
  59.6 119.0 %collective-permute-start.21 = (bf16[4,104,768]{2,1,0:T(8,128)(2,1)S(1)}, bf16[4,104,768]{2,1,0:T(8,128)(2,1)}, u32[]{:S(2)}, u32[]{:S(2)}) collective-permute-start(bf16[4,104,768]{2,1,0:T(8,128)(2,1)S(1)} %pad_maximum_fusion.6), channel_id=1, source_target_pairs={{0,2},{1,3},{2,0},{3,1},{4,6},{5,7},{6,4},{7,5},{8,10},{9,11},{10,... | collective-permute-start | bytes 1916936 | tf_op jit(solution)/shard_map/ppermute | solution.py:30
  61.1 111.1 %collective-permute-start.20 = (bf16[96,768]{1,0:T(8,128)(2,1)}, bf16[96,768]{1,0:T(8,128)(2,1)}, u32[]{:S(2)}, u32[]{:S(2)}) collective-permute-start(bf16[96,768]{1,0:T(8,128)(2,1)} %param.32), channel_id=1, source_target_pairs={{0,24},{4,28},{8,16},{12,20},{16,8},{20,12},{24,0},{28,4},{1,25},{... | collective-permute-start | bytes 442376 | tf_op jit(solution)/shard_map/ppermute | solution.py:38
  63.1 109.2 %collective-permute-start.19 = (bf16[96,768]{1,0:T(8,128)(2,1)}, bf16[96,768]{1,0:T(8,128)(2,1)}, u32[]{:S(2)}, u32[]{:S(2)}) collective-permute-start(bf16[96,768]{1,0:T(8,128)(2,1)} %param.32), channel_id=1, source_target_pairs={{0,16},{4,20},{8,24},{12,28},{16,0},{20,4},{24,8},{28,12},{1,17},{... | collective-permute-start | bytes 442376 | tf_op jit(solution)/shard_map/ppermute | solution.py:38
  63.2 109.1 %collective-permute-start.18 = (bf16[96,768]{1,0:T(8,128)(2,1)}, bf16[96,768]{1,0:T(8,128)(2,1)}, u32[]{:S(2)}, u32[]{:S(2)}) collective-permute-start(bf16[96,768]{1,0:T(8,128)(2,1)} %param.32), channel_id=1, source_target_pairs={{0,8},{4,12},{8,0},{12,4},{16,24},{20,28},{24,16},{28,20},{1,9},{5... | collective-permute-start | bytes 442376 | tf_op jit(solution)/shard_map/ppermute | solution.py:38
  174.1 16.4 %collective-permute-start.24 = (bf16[4,96,768]{2,1,0:T(8,128)(2,1)S(1)}, bf16[4,96,768]{2,1,0:T(8,128)(2,1)}, u32[]{:S(2)}, u32[]{:S(2)}) collective-permute-start(bf16[4,96,768]{2,1,0:T(8,128)(2,1)S(1)} %pad_maximum_fusion.7), channel_id=1, source_target_pairs={{0,4},{4,0},{8,12},{12,8},{16,20},{20,16},{24,28},{28,24},{1,5},{5... | collective-permute-start | bytes 1769480 | tf_op jit(solution)/shard_map/ppermute | solution.py:34
  174.9 18.8 %collective-permute-start.22 = (bf16[4,96,768]{2,1,0:T(8,128)(2,1)S(1)}, bf16[4,96,768]{2,1,0:T(8,128)(2,1)}, u32[]{:S(2)}, u32[]{:S(2)}) collective-permute-start(bf16[4,96,768]{2,1,0:T(8,128)(2,1)S(1)} %pad_maximum_fusion.7), channel_id=1, source_target_pairs={{0,2},{1,3},{2,0},{3,1},{4,6},{5,7},{6,4},{7,5},{8,10},{9,11},{10,... | collective-permute-start | bytes 1769480 | tf_op jit(solution)/shard_map/ppermute | solution.py:30
  177.9 20.1 %collective-permute-start.25 = (bf16[2,104,768]{2,1,0:T(8,128)(2,1)}, bf16[2,104,768]{2,1,0:T(8,128)(2,1)}, u32[]{:S(2)}, u32[]{:S(2)}) collective-permute-start(bf16[2,104,768]{2,1,0:T(8,128)(2,1)} %slice.453), channel_id=1, source_target_pairs={{0,2},{1,3},{2,0},{3,1},{4,6},{5,7},{6,4},{7,5},{8,10},{9,11},{10,... | collective-permute-start | bytes 958472 | tf_op jit(solution)/shard_map/ppermute | solution.py:30
  180.3 17.7 %collective-permute-start.27 = (bf16[2,104,768]{2,1,0:T(8,128)(2,1)}, bf16[2,104,768]{2,1,0:T(8,128)(2,1)}, u32[]{:S(2)}, u32[]{:S(2)}) collective-permute-start(bf16[2,104,768]{2,1,0:T(8,128)(2,1)} %slice.457), channel_id=1, source_target_pairs={{0,4},{4,0},{8,12},{12,8},{16,20},{20,16},{24,28},{28,24},{1,5},{5... | collective-permute-start | bytes 958472 | tf_op jit(solution)/shard_map/ppermute | solution.py:34
  182.8 18.3 %collective-permute-start.14 = (bf16[256,768]{1,0:T(8,128)(2,1)S(1)}, bf16[256,768]{1,0:T(8,128)(2,1)}, u32[]{:S(2)}, u32[]{:S(2)}) collective-permute-start(bf16[256,768]{1,0:T(8,128)(2,1)S(1)} %fusion.50), channel_id=1, source_target_pairs={{0,1},{1,0},{2,3},{3,2},{4,5},{5,4},{6,7},{7,6},{8,9},{9,8},{10,11... | collective-permute-start | bytes 1179656 | tf_op jit(solution)/shard_map/ppermute | solution.py:26
  192.2 10.8 %collective-permute-start.26 = (bf16[2,96,768]{2,1,0:T(8,128)(2,1)}, bf16[2,96,768]{2,1,0:T(8,128)(2,1)}, u32[]{:S(2)}, u32[]{:S(2)}) collective-permute-start(bf16[2,96,768]{2,1,0:T(8,128)(2,1)} %slice.456), channel_id=1, source_target_pairs={{0,2},{1,3},{2,0},{3,1},{4,6},{5,7},{6,4},{7,5},{8,10},{9,11},{10,... | collective-permute-start | bytes 884744 | tf_op jit(solution)/shard_map/ppermute | solution.py:30
  195.4 22.3 %collective-permute-start.28 = (bf16[2,96,768]{2,1,0:T(8,128)(2,1)}, bf16[2,96,768]{2,1,0:T(8,128)(2,1)}, u32[]{:S(2)}, u32[]{:S(2)}) collective-permute-start(bf16[2,96,768]{2,1,0:T(8,128)(2,1)} %slice.460), channel_id=1, source_target_pairs={{0,4},{4,0},{8,12},{12,8},{16,20},{20,16},{24,28},{28,24},{1,5},{5... | collective-permute-start | bytes 884744 | tf_op jit(solution)/shard_map/ppermute | solution.py:34
  247.1 50.6 %collective-permute-start.31 = (f32[256,768]{1,0:T(8,128)}, f32[256,768]{1,0:T(8,128)}, u32[]{:S(2)}, u32[]{:S(2)}) collective-permute-start(f32[256,768]{1,0:T(8,128)} %slice.467), channel_id=1, source_target_pairs={{0,1},{1,0},{2,3},{3,2},{4,5},{5,4},{6,7},{7,6},{8,9},{9,8},{10,11... | collective-permute-start | bytes 2359304 | tf_op jit(solution)/shard_map/ppermute | solution.py:26
  258.8 27.0 %collective-permute-start.43 = (bf16[2,96,768]{2,1,0:T(8,128)(2,1)}, bf16[2,96,768]{2,1,0:T(8,128)(2,1)}, u32[]{:S(2)}, u32[]{:S(2)}) collective-permute-start(bf16[2,96,768]{2,1,0:T(8,128)(2,1)} %bitcast.85), channel_id=1, source_target_pairs={{0,4},{4,0},{8,12},{12,8},{16,20},{20,16},{24,28},{28,24},{1,5},{5... | collective-permute-start | bytes 884744 | tf_op jit(solution)/shard_map/ppermute | solution.py:34
  264.6 24.5 %collective-permute-start.41 = (bf16[2,96,768]{2,1,0:T(8,128)(2,1)}, bf16[2,96,768]{2,1,0:T(8,128)(2,1)}, u32[]{:S(2)}, u32[]{:S(2)}) collective-permute-start(bf16[2,96,768]{2,1,0:T(8,128)(2,1)} %bitcast.81), channel_id=1, source_target_pairs={{0,2},{1,3},{2,0},{3,1},{4,6},{5,7},{6,4},{7,5},{8,10},{9,11},{10,... | collective-permute-start | bytes 884744 | tf_op jit(solution)/shard_map/ppermute | solution.py:30
  270.8 21.8 %collective-permute-start.50 = (bf16[2,96,768]{2,1,0:T(8,128)(2,1)}, bf16[2,96,768]{2,1,0:T(8,128)(2,1)}, u32[]{:S(2)}, u32[]{:S(2)}) collective-permute-start(bf16[2,96,768]{2,1,0:T(8,128)(2,1)} %bitcast.97), channel_id=1, source_target_pairs={{0,4},{4,0},{8,12},{12,8},{16,20},{20,16},{24,28},{28,24},{1,5},{5... | collective-permute-start | bytes 884744 | tf_op jit(solution)/shard_map/ppermute | solution.py:34
  275.9 19.2 %collective-permute-start.48 = (bf16[2,96,768]{2,1,0:T(8,128)(2,1)}, bf16[2,96,768]{2,1,0:T(8,128)(2,1)}, u32[]{:S(2)}, u32[]{:S(2)}) collective-permute-start(bf16[2,96,768]{2,1,0:T(8,128)(2,1)} %bitcast.93), channel_id=1, source_target_pairs={{0,2},{1,3},{2,0},{3,1},{4,6},{5,7},{6,4},{7,5},{8,10},{9,11},{10,... | collective-permute-start | bytes 884744 | tf_op jit(solution)/shard_map/ppermute | solution.py:30
  287.8 16.6 %collective-permute-start.44 = (bf16[4,96,768]{2,1,0:T(8,128)(2,1)}, bf16[4,96,768]{2,1,0:T(8,128)(2,1)}, u32[]{:S(2)}, u32[]{:S(2)}) collective-permute-start(bf16[4,96,768]{2,1,0:T(8,128)(2,1)} %pad_maximum_fusion.11), channel_id=1, source_target_pairs={{0,2},{1,3},{2,0},{3,1},{4,6},{5,7},{6,4},{7,5},{8,10},{9,11},{10,... | collective-permute-start | bytes 1769480 | tf_op jit(solution)/shard_map/ppermute | solution.py:30
  291.1 16.6 %collective-permute-start.42 = (bf16[4,96,768]{2,1,0:T(8,128)(2,1)}, bf16[4,96,768]{2,1,0:T(8,128)(2,1)}, u32[]{:S(2)}, u32[]{:S(2)}) collective-permute-start(bf16[4,96,768]{2,1,0:T(8,128)(2,1)} %pad_maximum_fusion.10), channel_id=1, source_target_pairs={{0,4},{4,0},{8,12},{12,8},{16,20},{20,16},{24,28},{28,24},{1,5},{5... | collective-permute-start | bytes 1769480 | tf_op jit(solution)/shard_map/ppermute | solution.py:34
  294.6 20.4 %collective-permute-start.51 = (bf16[4,96,768]{2,1,0:T(8,128)(2,1)}, bf16[4,96,768]{2,1,0:T(8,128)(2,1)}, u32[]{:S(2)}, u32[]{:S(2)}) collective-permute-start(bf16[4,96,768]{2,1,0:T(8,128)(2,1)} %pad_maximum_fusion.13), channel_id=1, source_target_pairs={{0,2},{1,3},{2,0},{3,1},{4,6},{5,7},{6,4},{7,5},{8,10},{9,11},{10,... | collective-permute-start | bytes 1769480 | tf_op jit(solution)/shard_map/ppermute | solution.py:30
  297.0 21.0 %collective-permute-start.49 = (bf16[4,96,768]{2,1,0:T(8,128)(2,1)}, bf16[4,96,768]{2,1,0:T(8,128)(2,1)}, u32[]{:S(2)}, u32[]{:S(2)}) collective-permute-start(bf16[4,96,768]{2,1,0:T(8,128)(2,1)} %pad_maximum_fusion.12), channel_id=1, source_target_pairs={{0,4},{4,0},{8,12},{12,8},{16,20},{20,16},{24,28},{28,24},{1,5},{5... | collective-permute-start | bytes 1769480 | tf_op jit(solution)/shard_map/ppermute | solution.py:34
  302.2 24.3 %collective-permute-start.32 = (bf16[256,768]{1,0:T(8,128)(2,1)S(1)}, bf16[256,768]{1,0:T(8,128)(2,1)S(1)}, u32[]{:S(2)}, u32[]{:S(2)}) collective-permute-start(bf16[256,768]{1,0:T(8,128)(2,1)S(1)} %get-tuple-element.106), channel_id=1, source_target_pairs={{0,1},{1,0},{2,3},{3,2},{4,5},{5,4},{6,7},{7,6},{8,9},{9,8},{10,11... | collective-permute-start | bytes 1179656 | tf_op jit(solution)/shard_map/ppermute | solution.py:26
  309.3 14.0 %collective-permute-start.47 = (bf16[96,768]{1,0:T(8,128)(2,1)S(1)}, bf16[96,768]{1,0:T(8,128)(2,1)S(1)}, u32[]{:S(2)}, u32[]{:S(2)}) collective-permute-start(bf16[96,768]{1,0:T(8,128)(2,1)S(1)} %get-tuple-element.128), channel_id=1, source_target_pairs={{0,24},{4,28},{8,16},{12,20},{16,8},{20,12},{24,0},{28,4},{1,25},{... | collective-permute-start | bytes 442376 | tf_op jit(solution)/shard_map/ppermute | solution.py:38
  311.3 12.0 %collective-permute-start.46 = (bf16[96,768]{1,0:T(8,128)(2,1)S(1)}, bf16[96,768]{1,0:T(8,128)(2,1)S(1)}, u32[]{:S(2)}, u32[]{:S(2)}) collective-permute-start(bf16[96,768]{1,0:T(8,128)(2,1)S(1)} %get-tuple-element.129), channel_id=1, source_target_pairs={{0,16},{4,20},{8,24},{12,28},{16,0},{20,4},{24,8},{28,12},{1,17},{... | collective-permute-start | bytes 442376 | tf_op jit(solution)/shard_map/ppermute | solution.py:38
  315.0 10.8 %collective-permute-start.45 = (bf16[96,768]{1,0:T(8,128)(2,1)S(1)}, bf16[96,768]{1,0:T(8,128)(2,1)S(1)}, u32[]{:S(2)}, u32[]{:S(2)}) collective-permute-start(bf16[96,768]{1,0:T(8,128)(2,1)S(1)} %get-tuple-element.127), channel_id=1, source_target_pairs={{0,8},{4,12},{8,0},{12,4},{16,24},{20,28},{24,16},{28,20},{1,9},{5... | collective-permute-start | bytes 442376 | tf_op jit(solution)/shard_map/ppermute | solution.py:38
  321.4 55.6 %collective-permute-start.54 = (bf16[96,768]{1,0:T(8,128)(2,1)}, bf16[96,768]{1,0:T(8,128)(2,1)}, u32[]{:S(2)}, u32[]{:S(2)}) collective-permute-start(bf16[96,768]{1,0:T(8,128)(2,1)} %get-tuple-element.121), channel_id=1, source_target_pairs={{0,24},{4,28},{8,16},{12,20},{16,8},{20,12},{24,0},{28,4},{1,25},{... | collective-permute-start | bytes 442376 | tf_op jit(solution)/shard_map/ppermute | solution.py:38
  323.3 54.0 %collective-permute-start.53 = (bf16[96,768]{1,0:T(8,128)(2,1)}, bf16[96,768]{1,0:T(8,128)(2,1)}, u32[]{:S(2)}, u32[]{:S(2)}) collective-permute-start(bf16[96,768]{1,0:T(8,128)(2,1)} %get-tuple-element.122), channel_id=1, source_target_pairs={{0,16},{4,20},{8,24},{12,28},{16,0},{20,4},{24,8},{28,12},{1,17},{... | collective-permute-start | bytes 442376 | tf_op jit(solution)/shard_map/ppermute | solution.py:38
  323.3 54.0 %collective-permute-start.52 = (bf16[96,768]{1,0:T(8,128)(2,1)}, bf16[96,768]{1,0:T(8,128)(2,1)}, u32[]{:S(2)}, u32[]{:S(2)}) collective-permute-start(bf16[96,768]{1,0:T(8,128)(2,1)} %get-tuple-element.120), channel_id=1, source_target_pairs={{0,8},{4,12},{8,0},{12,4},{16,24},{20,28},{24,16},{28,20},{1,9},{5... | collective-permute-start | bytes 442376 | tf_op jit(solution)/shard_map/ppermute | solution.py:38
  342.1 23.8 %collective-permute-start.36 = (bf16[2,96,768]{2,1,0:T(8,128)(2,1)}, bf16[2,96,768]{2,1,0:T(8,128)(2,1)}, u32[]{:S(2)}, u32[]{:S(2)}) collective-permute-start(bf16[2,96,768]{2,1,0:T(8,128)(2,1)} %get-tuple-element.135), channel_id=1, source_target_pairs={{0,4},{4,0},{8,12},{12,8},{16,20},{20,16},{24,28},{28,24},{1,5},{5... | collective-permute-start | bytes 884744 | tf_op jit(solution)/shard_map/ppermute | solution.py:34
  345.1 23.2 %collective-permute-start.34 = (bf16[2,96,768]{2,1,0:T(8,128)(2,1)}, bf16[2,96,768]{2,1,0:T(8,128)(2,1)}, u32[]{:S(2)}, u32[]{:S(2)}) collective-permute-start(bf16[2,96,768]{2,1,0:T(8,128)(2,1)} %get-tuple-element.134), channel_id=1, source_target_pairs={{0,2},{1,3},{2,0},{3,1},{4,6},{5,7},{6,4},{7,5},{8,10},{9,11},{10,... | collective-permute-start | bytes 884744 | tf_op jit(solution)/shard_map/ppermute | solution.py:30
  368.2 17.4 %collective-permute-start.37 = (bf16[4,96,768]{2,1,0:T(8,128)(2,1)}, bf16[4,96,768]{2,1,0:T(8,128)(2,1)}, u32[]{:S(2)}, u32[]{:S(2)}) collective-permute-start(bf16[4,96,768]{2,1,0:T(8,128)(2,1)} %pad_maximum_fusion.9), channel_id=1, source_target_pairs={{0,2},{1,3},{2,0},{3,1},{4,6},{5,7},{6,4},{7,5},{8,10},{9,11},{10,... | collective-permute-start | bytes 1769480 | tf_op jit(solution)/shard_map/ppermute | solution.py:30
  370.2 15.4 %collective-permute-start.35 = (bf16[4,96,768]{2,1,0:T(8,128)(2,1)}, bf16[4,96,768]{2,1,0:T(8,128)(2,1)}, u32[]{:S(2)}, u32[]{:S(2)}) collective-permute-start(bf16[4,96,768]{2,1,0:T(8,128)(2,1)} %pad_maximum_fusion.8), channel_id=1, source_target_pairs={{0,4},{4,0},{8,12},{12,8},{16,20},{20,16},{24,28},{28,24},{1,5},{5... | collective-permute-start | bytes 1769480 | tf_op jit(solution)/shard_map/ppermute | solution.py:34
  371.6 12.8 %all-to-all-start = ((f32[32,1,288]{2,1,0:T(1,128)}), f32[32,1,288]{2,1,0:T(1,128)S(1)}, u32[]{:S(2)}, u32[]{:S(2)}) async-start(f32[32,1,288]{2,1,0:T(1,128)} %copy.102), calls=%async_computation | async-start | bytes 98304 | tf_op jit(solution)/shard_map/all_to_all | solution.py:412
  377.0 14.9 %collective-permute-start.33 = (f32[256,768]{1,0:T(8,128)S(1)}, f32[256,768]{1,0:T(8,128)}, u32[]{:S(2)}, u32[]{:S(2)}) collective-permute-start(f32[256,768]{1,0:T(8,128)S(1)} %slice.469), channel_id=1, source_target_pairs={{0,1},{1,0},{2,3},{3,2},{4,5},{5,4},{6,7},{7,6},{8,9},{9,8},{10,11... | collective-permute-start | bytes 2359304 | tf_op jit(solution)/shard_map/ppermute | solution.py:26
  388.2 14.2 %collective-permute-start.39 = (bf16[96,768]{1,0:T(8,128)(2,1)S(1)}, bf16[96,768]{1,0:T(8,128)(2,1)S(1)}, u32[]{:S(2)}, u32[]{:S(2)}) collective-permute-start(bf16[96,768]{1,0:T(8,128)(2,1)S(1)} %get-tuple-element.118), channel_id=1, source_target_pairs={{0,16},{4,20},{8,24},{12,28},{16,0},{20,4},{24,8},{28,12},{1,17},{... | collective-permute-start | bytes 442376 | tf_op jit(solution)/shard_map/ppermute | solution.py:38
  389.6 12.8 %collective-permute-start.38 = (bf16[96,768]{1,0:T(8,128)(2,1)S(1)}, bf16[96,768]{1,0:T(8,128)(2,1)S(1)}, u32[]{:S(2)}, u32[]{:S(2)}) collective-permute-start(bf16[96,768]{1,0:T(8,128)(2,1)S(1)} %get-tuple-element.116), channel_id=1, source_target_pairs={{0,8},{4,12},{8,0},{12,4},{16,24},{20,28},{24,16},{28,20},{1,9},{5... | collective-permute-start | bytes 442376 | tf_op jit(solution)/shard_map/ppermute | solution.py:38
  (112 other events, 640.4 us)
